TPU v7x, 32 devices: a whole 2x2x4 slice. The times are simulated.
32 devices in a mesh: space: 16 (over z, x, core), tm: 2 (over y).
Axes of the slice: x: 2, y: 2, z: 4, core: 2. Of those that a mesh axis runs over, the one named last changes fastest.
Arguments:
- node_feats: bfloat16 [128, 7168, 128], P('tm', 'space'), may hold values from -6 to 6
- positions: float32 [128, 3, 7168], P('tm', None, 'space'), may hold values from -3 to 3
- neighbours: int32 [128, 224, 8], P('tm', 'space'), may hold values from 0 to 223, as said below
- edge_in: bfloat16 [256, 128], replicated, may hold values from -0.375 to 0.375
- edge_out: bfloat16 [128, 128], replicated, may hold values from -0.5 to 0.5
- edge_params: float32 [3, 128], replicated, may hold values from -3 to 3
- coord_weight: float32 [128], replicated, may hold values from -0.5 to 0.5
- spectral: bfloat16 [2, 64, 128, 128], replicated, may hold values from -0.375 to 0.375
- node_in: bfloat16 [256, 128], replicated, may hold values from -0.375 to 0.375
- node_out: bfloat16 [128, 128], replicated, may hold values from -0.5 to 0.5
- node_bias: float32 [2, 128], replicated, may hold values from -3 to 3
Outputs:
- new_feats: bfloat16 [128, 7168, 128], P('tm', 'space')
- new_positions: float32 [128, 3, 7168], P('tm', None, 'space')
Inputs may be any that keep to these rules, and one draw needn't show every extreme that they name: neighbours[f, b, s] = (b + o) mod 224 for an offset o with -6 <= o <= 6; the offsets of a block's list may repeat, and every list holds the offsets 0, -6 and +6 in some slots.
All inputs are finite; a program needn't handle non-finite values.
Results may differ from a plain program's by a relative error of at most 0.0065.
Values may be sent and summed in bfloat16 or wider, within the bound.
No kernel may reach another device: no remote copies, remote signals or barrier semaphores. Data moves between devices by JAX's collectives and lax.ppermute only.
A program may use at most 320 MiB of HBM per device.

v0:
```python
import math
import jax
import jax.numpy as jnp
from jax import lax
from jax.sharding import PartitionSpec as P

BLOCK = 32
GHOST = 6


def with_halo(block, sides, width):
    for axis, dim in sides:
        count = lax.axis_size(axis)
        forward = [(i, i + 1) for i in range(count - 1)]
        forward.append((count - 1, 0))
        backward = [(target, source) for source, target in forward]
        low = lax.ppermute(
            lax.slice_in_dim(block, block.shape[dim] - width, None, axis=dim), axis, forward
        )
        high = lax.ppermute(lax.slice_in_dim(block, 0, width, axis=dim), axis, backward)
        block = jnp.concatenate([low, block, high], axis=dim)
    return block


def split_parts(values):
    high_part = values.astype(jnp.bfloat16)
    low_part = (values - high_part.astype(jnp.float32)).astype(jnp.bfloat16)
    return (high_part, low_part)


def edge_pass(own_src, other_dst, own_pos, other_pos, picked, edge_out, edge_params, coord_weight):
    frames, own_blocks, block_len, feat_width = own_src.shape
    other_blocks = other_dst.shape[1]
    flat_dst = other_dst.reshape(frames, other_blocks, block_len * feat_width)
    dst_high, dst_low = split_parts(flat_dst)
    block_ids = jnp.arange(other_blocks, dtype=jnp.int32)
    summed = jnp.zeros(own_src.shape, jnp.float32)
    moved = jnp.zeros(own_pos.shape, jnp.float32)
    for slot_num in range(picked.shape[2]):
        chosen = picked[:, :, slot_num]
        select_f32 = (chosen[:, :, None] == block_ids[None, None, :]).astype(jnp.float32)
        select_bf = select_f32.astype(jnp.bfloat16)
        near_dst = jnp.einsum(
            "fbc,fcx->fbx", select_bf, dst_high, preferred_element_type=jnp.float32
        ) + jnp.einsum("fbc,fcx->fbx", select_bf, dst_low, preferred_element_type=jnp.float32)
        near_dst = near_dst.reshape(own_src.shape)
        near_pos = jnp.einsum(
            "fbc,fdcl->fdbl", select_f32, other_pos, precision=lax.Precision.HIGHEST
        )
        offset_vec = own_pos - near_pos
        dist_sq = jnp.sum(offset_vec * offset_vec, axis=1)
        pre_act = own_src + near_dst + edge_params[0] + dist_sq[..., None] * edge_params[1]
        hidden = jax.nn.silu(pre_act).astype(jnp.bfloat16)
        out_act = (
            jnp.dot(
                hidden.reshape(-1, feat_width), edge_out, preferred_element_type=jnp.float32
            ).reshape(pre_act.shape)
            + edge_params[2]
        )
        message = jax.nn.silu(out_act)
        summed = summed + message
        weight = jnp.sum(message * coord_weight, axis=-1) / (1.0 + jnp.sqrt(dist_sq + 1.0))
        moved = moved + offset_vec * weight[:, None]
    return (summed, moved)


def spectral_conv(msg_block, spectral, out_count):
    frame_count, item_count, feat_width = msg_block.shape
    mode_count = spectral.shape[1]
    mode_ids = jnp.arange(mode_count, dtype=jnp.int32)
    time_ids = jnp.arange(frame_count, dtype=jnp.int32)
    step_angle = 2.0 * math.pi / frame_count
    angles = (mode_ids[:, None] * time_ids[None, :] % frame_count).astype(jnp.float32) * step_angle
    forward = jnp.concatenate([jnp.cos(angles), -jnp.sin(angles)], axis=0)
    fwd_high, fwd_low = split_parts(forward)
    flat_msg = msg_block.reshape(frame_count, -1)
    coeffs = jnp.dot(fwd_high, flat_msg, preferred_element_type=jnp.float32) + jnp.dot(
        fwd_low, flat_msg, preferred_element_type=jnp.float32
    )
    coeffs = coeffs.astype(jnp.bfloat16).reshape(2, mode_count, item_count, feat_width)
    mixed_real = jnp.einsum(
        "knh,khg->kng", coeffs[0], spectral[0], preferred_element_type=jnp.float32
    ) - jnp.einsum("knh,khg->kng", coeffs[1], spectral[1], preferred_element_type=jnp.float32)
    mixed_imag = jnp.einsum(
        "knh,khg->kng", coeffs[0], spectral[1], preferred_element_type=jnp.float32
    ) + jnp.einsum("knh,khg->kng", coeffs[1], spectral[0], preferred_element_type=jnp.float32)
    out_times = jnp.arange(out_count, dtype=jnp.int32)
    back_angles = (out_times[:, None] * mode_ids[None, :] % frame_count).astype(
        jnp.float32
    ) * step_angle
    weights = (jnp.where(mode_ids == 0, 1.0, 2.0) / frame_count).astype(jnp.float32)
    inverse = jnp.concatenate(
        [jnp.cos(back_angles) * weights, -jnp.sin(back_angles) * weights], axis=1
    )
    inv_high, inv_low = split_parts(inverse)
    mixed_all = jnp.concatenate([mixed_real, mixed_imag], axis=0).reshape(2 * mode_count, -1)
    mix_high, mix_low = split_parts(mixed_all)
    conv_out = (
        jnp.dot(inv_high, mix_high, preferred_element_type=jnp.float32)
        + jnp.dot(inv_low, mix_high, preferred_element_type=jnp.float32)
        + jnp.dot(inv_high, mix_low, preferred_element_type=jnp.float32)
    )
    return conv_out.astype(jnp.bfloat16).reshape(out_count, item_count, feat_width)


def shards(
    node_feats,
    positions,
    neighbours,
    edge_in,
    edge_out,
    edge_params,
    coord_weight,
    spectral,
    node_in,
    node_out,
    node_bias,
):
    frames, local_rows, feat_width = node_feats.shape
    blocks = local_rows // BLOCK
    rim_rows = GHOST * BLOCK
    slot_count = neighbours.shape[2]
    slab_index = lax.axis_index("space")
    total_blocks = blocks * lax.axis_size("space")
    first_block = slab_index * blocks - GHOST
    ext_feats = with_halo(node_feats, (("space", 1),), rim_rows)
    ext_pos = with_halo(positions.astype(jnp.bfloat16), (("space", 2),), rim_rows).astype(
        positions.dtype
    )
    ext_pos4 = ext_pos.reshape(frames, 3, blocks + 2 * GHOST, BLOCK)
    own_src = jnp.dot(node_feats, edge_in[:feat_width], preferred_element_type=jnp.float32).reshape(
        frames, blocks, BLOCK, feat_width
    )
    own_pos = positions.reshape(frames, 3, blocks, BLOCK)
    picked = (neighbours - first_block) % total_blocks
    ext_dst = jnp.dot(ext_feats, edge_in[feat_width:], preferred_element_type=jnp.float32).reshape(
        frames, blocks + 2 * GHOST, BLOCK, feat_width
    )
    summed, moved = edge_pass(
        own_src, ext_dst, own_pos, ext_pos4, picked, edge_out, edge_params, coord_weight
    )
    mean_msg = (summed / slot_count).astype(jnp.bfloat16).reshape(frames, local_rows, feat_width)
    new_positions = positions + (moved / slot_count).reshape(frames, 3, local_rows)
    regrouped = lax.all_to_all(mean_msg, "tm", split_axis=1, concat_axis=0, tiled=True)
    conv_all = spectral_conv(regrouped, spectral, regrouped.shape[0])
    conv_own = lax.all_to_all(conv_all, "tm", split_axis=0, concat_axis=1, tiled=True)
    node_pre = (
        jnp.dot(node_feats, node_in[:feat_width], preferred_element_type=jnp.float32)
        + jnp.dot(conv_own, node_in[feat_width:], preferred_element_type=jnp.float32)
        + node_bias[0]
    )
    node_hidden = jax.nn.silu(node_pre).astype(jnp.bfloat16)
    new_feats = (
        node_feats.astype(jnp.float32)
        + (jnp.dot(node_hidden, node_out, preferred_element_type=jnp.float32) + node_bias[1])
    ).astype(jnp.bfloat16)
    return (new_feats, new_positions)


def solution(mesh):
    placed = (
        P("tm", "space", None),
        P("tm", None, "space"),
        P("tm", "space", None),
        P(),
        P(),
        P(),
        P(),
        P(),
        P(),
        P(),
        P(),
    )
    return jax.shard_map(
        shards,
        mesh=mesh,
        in_specs=placed,
        out_specs=(P("tm", "space", None), P("tm", None, "space")),
        check_vma=False,
    )
```

profile of v0, /device:TPU:1, one launch (start us, length us, event | category | flops | bytes accessed | tf_op | source)
XLA Modules:
  0.0 959.1 jit_solution(7866914278327090848)
XLA Ops:
  0.7 6.1 fusion.134
  6.7 2.6 collective-permute-start
  14.3 10.3 %fusion.99 = f32[64,448,128]{2,1,0:T(8,128)} fusion(bf16[64,448,128]{2,1,0:T(8,128)(2,1)} %param.11, bf16[256,128]{1,0:T(8,128)(2,1)S(1)} %copy-done.48), kind=kOutput, calls=%fused_computation.187 | convolution fusion | flops 939524096 | bytes 22052864 | tf_op jit(solution)/shard_map/dot_general | solution.py:131
  26.8 53.9 %collective-permute-done.2 = bf16[64,3,192]{0,2,1:T(8,128)(2,1)S(1)} collective-permute-done((bf16[64,3,192]{0,2,1:T(8,128)(2,1)}, bf16[64,3,192]{0,2,1:T(8,128)(2,1)S(1)}, u32[]{:S(2)}, u32[]{:S(2)}) %collective-permute-start.2) | collective-permute-done | bytes 73760 | tf_op jit(solution)/shard_map/ppermute | solution.py:17
  91.4 2.5 multiply_reduce_fusion.10
  96.3 2.5 multiply_reduce_fusion.12
  103.7 2.5 multiply_reduce_fusion.15
  106.3 13.9 %fusion.3 = f32[64,832,128]{2,1,0:T(8,128)} fusion(bf16[64,192,128]{2,1,0:T(8,128)(2,1)} %collective-permute-done.1, bf16[64,448,128]{2,1,0:T(8,128)(2,1)} %param.11, bf16[64,192,128]{2,1,0:T(8,128)(2,1)} %collective-permute-done, bf16[256,128]{1,0:T(8,128)(2,1)S(1)} %copy-done.48), kind=kOutput, calls=%fused_computation.37 | convolution fusion | flops 1785724928 | bytes 40927232 | tf_op jit(solution)/shard_map/dot_general | solution.py:136
  120.1 28.5 %reshape_reshape.3 = f32[64,26,4096]{2,1,0:T(8,128)} reshape(f32[64,832,128]{2,1,0:T(8,128)} %fusion.3) | data formatting | bytes 54525952 | tf_op jit(solution)/shard_map/reshape;reshape | solution.py:34
  148.6 29.6 %subtract_convert_fusion = (bf16[64,26,4096]{2,1,0:T(8,128)(2,1)}, bf16[64,26,4096]{2,1,0:T(8,128)(2,1)S(1)}) fusion(f32[64,26,4096]{2,1,0:T(8,128)} %reshape_reshape.3), kind=kLoop, calls=%fused_computation.5 | loop fusion | flops 27262976 | bytes 54525952 | tf_op jit(solution)/shard_map/convert_element_type | solution.py:27
  178.2 7.1 fusion.52
  185.3 7.1 fusion.51
  192.3 7.1 fusion.50
  199.4 7.4 fusion.49
  206.8 7.2 fusion.48
  214.0 7.1 fusion.47
  221.0 7.1 fusion.46
  228.2 7.1 fusion.45
  235.3 18.9 %convolution_add_fusion.3 = f32[64,14,4096]{2,1,0:T(8,128)} fusion(f32[64,14,4096]{2,1,0:T(8,128)} %fusion.52, bf16[64,26,4096]{2,1,0:T(8,128)(2,1)} %get-tuple-element.18, s32[64,14]{1,0:T(8,128)S(1)} %copy.208), kind=kOutput, calls=%fused_computation.46 | convolution fusion | flops 194580736 | bytes 42995200 | tf_op jit(solution)/shard_map/fbc,fcx->fbx/dot_general | solution.py:45
  254.2 17.9 %reshape.371 = f32[64,14,32,128]{3,2,1,0:T(8,128)} reshape(f32[64,14,4096]{2,1,0:T(8,128)} %convolution_add_fusion.3) | data formatting | bytes 29360128 | tf_op jit(solution)/shard_map/reshape | solution.py:46
  272.1 18.9 %convolution_add_fusion.4 = f32[64,14,4096]{2,1,0:T(8,128)} fusion(f32[64,14,4096]{2,1,0:T(8,128)} %fusion.51, bf16[64,26,4096]{2,1,0:T(8,128)(2,1)} %get-tuple-element.18, s32[64,14]{1,0:T(8,128)S(1)} %copy.203), kind=kOutput, calls=%fused_computation.47 | convolution fusion | flops 194580736 | bytes 42995200 | tf_op jit(solution)/shard_map/fbc,fcx->fbx/dot_general | solution.py:45
  290.9 17.5 %reshape.370 = f32[64,14,32,128]{3,2,1,0:T(8,128)} reshape(f32[64,14,4096]{2,1,0:T(8,128)} %convolution_add_fusion.4) | data formatting | bytes 29360128 | tf_op jit(solution)/shard_map/reshape | solution.py:46
  308.4 18.9 %convolution_add_fusion.5 = f32[64,14,4096]{2,1,0:T(8,128)} fusion(f32[64,14,4096]{2,1,0:T(8,128)} %fusion.50, bf16[64,26,4096]{2,1,0:T(8,128)(2,1)} %get-tuple-element.18, s32[64,14]{1,0:T(8,128)S(1)} %copy.198), kind=kOutput, calls=%fused_computation.48 | convolution fusion | flops 194580736 | bytes 42995200 | tf_op jit(solution)/shard_map/fbc,fcx->fbx/dot_general | solution.py:45
  327.3 17.5 %reshape.369 = f32[64,14,32,128]{3,2,1,0:T(8,128)} reshape(f32[64,14,4096]{2,1,0:T(8,128)} %convolution_add_fusion.5) | data formatting | bytes 29360128 | tf_op jit(solution)/shard_map/reshape | solution.py:46
  344.8 19.0 %convolution_add_fusion.6 = f32[64,14,4096]{2,1,0:T(8,128)} fusion(f32[64,14,4096]{2,1,0:T(8,128)} %fusion.49, bf16[64,26,4096]{2,1,0:T(8,128)(2,1)} %get-tuple-element.18, s32[64,14]{1,0:T(8,128)S(1)} %copy-done.40), kind=kOutput, calls=%fused_computation.49 | convolution fusion | flops 194580736 | bytes 42995200 | tf_op jit(solution)/shard_map/fbc,fcx->fbx/dot_general | solution.py:45
  363.8 17.6 %reshape.368 = f32[64,14,32,128]{3,2,1,0:T(8,128)} reshape(f32[64,14,4096]{2,1,0:T(8,128)} %convolution_add_fusion.6) | data formatting | bytes 29360128 | tf_op jit(solution)/shard_map/reshape | solution.py:46
  381.4 19.0 %convolution_add_fusion.7 = f32[64,14,4096]{2,1,0:T(8,128)} fusion(f32[64,14,4096]{2,1,0:T(8,128)} %fusion.48, bf16[64,26,4096]{2,1,0:T(8,128)(2,1)} %get-tuple-element.18, s32[64,14]{1,0:T(8,128)S(1)} %copy-done.38), kind=kOutput, calls=%fused_computation.50 | convolution fusion | flops 194580736 | bytes 42995200 | tf_op jit(solution)/shard_map/fbc,fcx->fbx/dot_general | solution.py:45
  400.4 17.5 %reshape.367 = f32[64,14,32,128]{3,2,1,0:T(8,128)} reshape(f32[64,14,4096]{2,1,0:T(8,128)} %convolution_add_fusion.7) | data formatting | bytes 29360128 | tf_op jit(solution)/shard_map/reshape | solution.py:46
  417.9 18.9 %convolution_add_fusion.8 = f32[64,14,4096]{2,1,0:T(8,128)} fusion(f32[64,14,4096]{2,1,0:T(8,128)} %fusion.47, bf16[64,26,4096]{2,1,0:T(8,128)(2,1)} %get-tuple-element.18, s32[64,14]{1,0:T(8,128)S(1)} %copy-done.36), kind=kOutput, calls=%fused_computation.51 | convolution fusion | flops 194580736 | bytes 42995200 | tf_op jit(solution)/shard_map/fbc,fcx->fbx/dot_general | solution.py:45
  436.7 17.5 %reshape.366 = f32[64,14,32,128]{3,2,1,0:T(8,128)} reshape(f32[64,14,4096]{2,1,0:T(8,128)} %convolution_add_fusion.8) | data formatting | bytes 29360128 | tf_op jit(solution)/shard_map/reshape | solution.py:46
  454.2 18.9 %convolution_add_fusion.9 = f32[64,14,4096]{2,1,0:T(8,128)} fusion(f32[64,14,4096]{2,1,0:T(8,128)} %fusion.46, bf16[64,26,4096]{2,1,0:T(8,128)(2,1)} %get-tuple-element.18, s32[64,14]{1,0:T(8,128)S(1)} %copy-done.34), kind=kOutput, calls=%fused_computation.52 | convolution fusion | flops 194580736 | bytes 42995200 | tf_op jit(solution)/shard_map/fbc,fcx->fbx/dot_general | solution.py:45
  473.1 17.7 %reshape.365 = f32[64,14,32,128]{3,2,1,0:T(8,128)} reshape(f32[64,14,4096]{2,1,0:T(8,128)} %convolution_add_fusion.9) | data formatting | bytes 29360128 | tf_op jit(solution)/shard_map/reshape | solution.py:46
  490.8 18.9 %convolution_add_fusion.10 = f32[64,14,4096]{2,1,0:T(8,128)} fusion(f32[64,14,4096]{2,1,0:T(8,128)} %fusion.45, bf16[64,26,4096]{2,1,0:T(8,128)(2,1)} %get-tuple-element.18, s32[64,14]{1,0:T(8,128)S(1)} %copy-done.32), kind=kOutput, calls=%fused_computation.53 | convolution fusion | flops 194580736 | bytes 42995200 | tf_op jit(solution)/shard_map/fbc,fcx->fbx/dot_general | solution.py:45
  509.7 17.6 %reshape.364 = f32[64,14,32,128]{3,2,1,0:T(8,128)} reshape(f32[64,14,4096]{2,1,0:T(8,128)} %convolution_add_fusion.10) | data formatting | bytes 29360128 | tf_op jit(solution)/shard_map/reshape | solution.py:46
  527.5 20.7 %divide_multiply_fusion = f32[64,14,32,128]{3,2,1,0:T(8,128)} fusion(f32[128]{0:T(128)S(1)} %copy-done.53, f32[64,14,32,128]{3,2,1,0:T(8,128)} %bitcast.227, f32[64,14,32,128]{3,2,1,0:T(8,128)} %reshape.371, f32[64,14,32]{2,1,0:T(8,128)S(1)} %copy-done.16, f32[128]{0:T(128)S(1)} %copy-done.54, f32[128]{0:T(128)S(1)} %copy-done.52, ...), kind=kOutput, calls=%fused_computation.21 | convolution fusion | flops 990904320 | bytes 44189184 | tf_op jit(solution)/shard_map/dot_general | solution.py:55
  548.2 16.6 %divide_multiply_fusion.1 = f32[64,14,32,128]{3,2,1,0:T(8,128)} fusion(f32[128]{0:T(128)S(1)} %copy-done.53, f32[64,14,32,128]{3,2,1,0:T(8,128)S(1)} %bitcast.231, f32[64,14,32,128]{3,2,1,0:T(8,128)} %reshape.370, f32[64,14,32]{2,1,0:T(8,128)S(1)} %copy-done.18, f32[128]{0:T(128)S(1)} %copy-done.54, f32[128]{0:T(128)S(1)} %copy-done.52, ...), kind=kOutput, calls=%fused_computation.23 | convolution fusion | flops 990904320 | bytes 44189184 | tf_op jit(solution)/shard_map/dot_general | solution.py:55
  564.9 10.9 %divide_multiply_fusion.2 = f32[64,14,32,128]{3,2,1,0:T(8,128)} fusion(f32[128]{0:T(128)S(1)} %copy-done.53, f32[64,14,32,128]{3,2,1,0:T(8,128)S(1)} %bitcast.232, f32[64,14,32,128]{3,2,1,0:T(8,128)S(1)} %bitcast.243, f32[64,14,32]{2,1,0:T(8,128)S(1)} %copy-done.20, f32[128]{0:T(128)S(1)} %copy-done.54, f32[128]{0:T(128)S(1)} %copy-done.52, ...), kind=kOutput, calls=%fused_computation.25 | convolution fusion | flops 990904320 | bytes 44189184 | tf_op jit(solution)/shard_map/dot_general | solution.py:55
  575.8 17.8 %divide_multiply_fusion.3 = f32[64,14,32,128]{3,2,1,0:T(8,128)} fusion(f32[128]{0:T(128)S(1)} %copy-done.53, f32[64,14,32,128]{3,2,1,0:T(8,128)S(1)} %bitcast.233, f32[64,14,32,128]{3,2,1,0:T(8,128)} %reshape.368, f32[64,14,32]{2,1,0:T(8,128)S(1)} %copy-done.22, f32[128]{0:T(128)S(1)} %copy-done.54, f32[128]{0:T(128)S(1)} %copy-done.52, ...), kind=kOutput, calls=%fused_computation.27 | convolution fusion | flops 990904320 | bytes 44189184 | tf_op jit(solution)/shard_map/dot_general | solution.py:55
  593.6 10.9 %divide_multiply_fusion.4 = f32[64,14,32,128]{3,2,1,0:T(8,128)} fusion(f32[128]{0:T(128)S(1)} %copy-done.53, f32[64,14,32,128]{3,2,1,0:T(8,128)S(1)} %bitcast.234, f32[64,14,32,128]{3,2,1,0:T(8,128)S(1)} %copy-done.4, f32[64,14,32]{2,1,0:T(8,128)S(1)} %copy-done.24, f32[128]{0:T(128)S(1)} %copy-done.54, f32[128]{0:T(128)S(1)} %copy-done.52, ...), kind=kOutput, calls=%fused_computation.29 | convolution fusion | flops 990904320 | bytes 44189184 | tf_op jit(solution)/shard_map/dot_general | solution.py:55
  604.5 17.8 %divide_multiply_fusion.5 = f32[64,14,32,128]{3,2,1,0:T(8,128)} fusion(f32[128]{0:T(128)S(1)} %copy-done.53, f32[64,14,32,128]{3,2,1,0:T(8,128)S(1)} %bitcast.235, f32[64,14,32,128]{3,2,1,0:T(8,128)} %reshape.366, f32[64,14,32]{2,1,0:T(8,128)S(1)} %copy-done.26, f32[128]{0:T(128)S(1)} %copy-done.54, f32[128]{0:T(128)S(1)} %copy-done.52, ...), kind=kOutput, calls=%fused_computation.31 | convolution fusion | flops 990904320 | bytes 44189184 | tf_op jit(solution)/shard_map/dot_general | solution.py:55
  622.4 10.9 %divide_multiply_fusion.6 = f32[64,14,32,128]{3,2,1,0:T(8,128)} fusion(f32[128]{0:T(128)S(1)} %copy-done.53, f32[64,14,32,128]{3,2,1,0:T(8,128)S(1)} %bitcast.236, f32[64,14,32,128]{3,2,1,0:T(8,128)S(1)} %copy-done.5, f32[64,14,32]{2,1,0:T(8,128)S(1)} %copy-done.28, f32[128]{0:T(128)S(1)} %copy-done.54, f32[128]{0:T(128)S(1)} %copy-done.52, ...), kind=kOutput, calls=%fused_computation.33 | convolution fusion | flops 990904320 | bytes 44189184 | tf_op jit(solution)/shard_map/dot_general | solution.py:55
  633.2 52.7 %multiply_reduce_fusion.7 = (f32[64,14,32]{2,1,0:T(8,128)}, f32[64,14,32]{2,1,0:T(8,128)}, f32[64,14,32]{2,1,0:T(8,128)}, f32[64,14,32]{2,1,0:T(8,128)}, f32[64,...) fusion(f32[128]{0:T(128)S(1)} %copy-done.56, ...), kind=kOutput, calls=%fused_computation.17 | convolution fusion | flops 1082425344 | bytes 140527616 | tf_op jit(solution)/shard_map/dot_general | solution.py:55
  685.9 10.8 %copy.213 = bf16[64,448,128]{2,0,1:T(8,128)(2,1)} copy(bf16[64,448,128]{2,1,0:T(8,128)(2,1)} %bitcast.245) | data formatting | bytes 14680064 | tf_op jit(solution)/shard_map/reshape | solution.py:142
  696.8 6.8 all-to-all-start
  703.8 47.5 %all-to-all-done = bf16[64,448,128]{2,0,1:T(8,128)(2,1)} async-done(((bf16[64,448,128]{2,0,1:T(8,128)(2,1)}), bf16[64,448,128]{2,0,1:T(8,128)(2,1)}, u32[]{:S(2)}, u32[]{:S(2)}) %all-to-all-start) | async-done | bytes 7340064 | tf_op jit(solution)/shard_map/all_to_all | solution.py:144
  751.3 7.8 copy.215
  759.1 3.0 copy-done.2
  762.2 8.1 fusion.11
  770.3 13.5 %fusion = bf16[128,28672]{1,0:T(8,128)(2,1)} fusion(f32[128,28672]{1,0:T(8,128)} %fusion.11, bf16[16,8,224,128]{3,2,1,0:T(8,128)(2,1)} %bitcast.226, f32[64,128]{1,0:T(8,128)S(1)} %get-tuple-element.66, f32[64,128]{1,0:T(8,128)S(1)} %get-tuple-element.67), kind=kOutput, calls=%fused_computation.3 | convolution fusion | flops 946946048 | bytes 29425664 | tf_op jit(solution)/shard_map/dot_general | solution.py:77
  783.8 3.8 slice_bitcast_fusion
  791.7 4.0 convolution_subtract_fusion
  795.7 4.2 convolution_add_fusion.11
  799.9 6.5 pad_maximum_fusion
  806.4 5.2 copy-done.1
  811.6 14.5 %fusion.15 = f32[128,28672]{1,0:T(8,128)} fusion(f32[16,8,224,128]{3,2,1,0:T(8,128)S(1)} %bitcast.222, f32[128,64]{0,1:T(8,128)S(1)} %get-tuple-element.41, f32[128,64]{0,1:T(8,128)S(1)} %get-tuple-element.40), kind=kOutput, calls=%fused_computation.56 | convolution fusion | flops 939589632 | bytes 29425664 | tf_op jit(solution)/shard_map/dot_general | solution.py:99
  826.1 24.5 %convolution_add_fusion.1 = f32[128,28672]{1,0:T(8,128)} fusion(f32[128,28672]{1,0:T(8,128)} %fusion.15, f32[16,8,224,128]{3,2,1,0:T(8,128)} %bitcast.223, f32[128,64]{0,1:T(8,128)S(1)} %get-tuple-element.41, f32[128,64]{0,1:T(8,128)S(1)} %get-tuple-element.40), kind=kOutput, calls=%fused_computation.1 | convolution fusion | flops 943276032 | bytes 44105728 | tf_op jit(solution)/shard_map/dot_general | solution.py:100
  850.6 22.7 %fusion.16 = bf16[16,8,224,128]{3,1,2,0:T(8,128)(2,1)} fusion(f32[128,28672]{1,0:T(8,128)} %convolution_add_fusion.1, f32[16,8,224,128]{3,2,1,0:T(8,128)} %bitcast.224, f32[128,64]{0,1:T(8,128)S(1)} %get-tuple-element.41, f32[128,64]{0,1:T(8,128)S(1)} %get-tuple-element.40), kind=kOutput, calls=%fused_computation.57 | convolution fusion | flops 961609728 | bytes 36765696 | tf_op jit(solution)/shard_map/dot_general | solution.py:101
  873.3 7.8 copy.242
  881.1 6.6 all-to-all-start.1
  888.0 12.7 %fusion.101 = f32[64,448,128]{2,1,0:T(8,128)} fusion(bf16[64,448,128]{2,1,0:T(8,128)(2,1)} %param.11, bf16[256,128]{1,0:T(8,128)(2,1)S(1)} %copy-done.49), kind=kOutput, calls=%fused_computation.189 | convolution fusion | flops 939524096 | bytes 22052864 | tf_op jit(solution)/shard_map/dot_general | solution.py:148
  906.1 3.6 add_multiply_fusion
  911.4 25.3 %all-to-all-done.1 = bf16[128,224,128]{2,1,0:T(8,128)(2,1)} async-done(((bf16[128,224,128]{2,1,0:T(8,128)(2,1)}), bf16[128,224,128]{2,1,0:T(8,128)(2,1)}, u32[]{:S(2)}, u32[]{:S(2)}) %all-to-all-start.1) | async-done | bytes 7340064 | tf_op jit(solution)/shard_map/all_to_all | solution.py:146
  936.7 7.2 copy.216
  943.9 14.9 %add_convert_fusion = bf16[64,448,128]{2,1,0:T(8,128)(2,1)} fusion(bf16[64,448,128]{2,1,0:T(8,128)(2,1)} %param.11, f32[128]{0:T(128)S(1)} %get-tuple-element.39, f32[64,448,128]{2,1,0:T(8,128)} %fusion.101, bf16[64,448,128]{2,1,0:T(8,128)(2,1)} %bitcast.246, f32[128]{0:T(128)S(1)} %get-tuple-element.38, bf16[128,128]{1,0:T(8,128)(2,1)S(1)} %copy-done.55, ...), kind=kOutput, calls=%fused_computation.18 | convolution fusion | flops 1919418368 | bytes 36766720 | tf_op jit(solution)/shard_map/dot_general | solution.py:155
  (173 shorter events, 36.6 us)
Async XLA Ops:
  0.6 526.7 %copy-start = (bf16[128,128]{1,0:T(8,128)(2,1)S(1)}, bf16[128,128]{1,0:T(8,128)(2,1)}, u32[]{:S(2)}) copy-start(bf16[128,128]{1,0:T(8,128)(2,1)} %param.15) | copy-start | bytes 98308
  0.6 13.7 %copy-start.48 = (bf16[256,128]{1,0:T(8,128)(2,1)S(1)}, bf16[256,128]{1,0:T(8,128)(2,1)}, u32[]{:S(2)}) copy-start(bf16[256,128]{1,0:T(8,128)(2,1)} %param.14) | copy-start | bytes 196612
  6.7 99.5 %collective-permute-start = (bf16[64,192,128]{2,1,0:T(8,128)(2,1)}, bf16[64,192,128]{2,1,0:T(8,128)(2,1)}, u32[]{:S(2)}, u32[]{:S(2)}) collective-permute-start(bf16[64,192,128]{2,1,0:T(8,128)(2,1)} %get-tuple-element.23), channel_id=1, source_target_pairs={{0,2},{2,4},{4,6},{6,8},{8,10},{10,12},{12,14},{14,16},{16,18},{18... | collective-permute-start | bytes 9437192 | tf_op jit(solution)/shard_map/ppermute | solution.py:17
  9.3 96.9 %collective-permute-start.1 = (bf16[64,192,128]{2,1,0:T(8,128)(2,1)}, bf16[64,192,128]{2,1,0:T(8,128)(2,1)}, u32[]{:S(2)}, u32[]{:S(2)}) collective-permute-start(bf16[64,192,128]{2,1,0:T(8,128)(2,1)} %get-tuple-element.24), channel_id=1, source_target_pairs={{2,0},{4,2},{6,4},{8,6},{10,8},{12,10},{14,12},{16,14},{18,16},{20... | collective-permute-start | bytes 9437192 | tf_op jit(solution)/shard_map/ppermute | solution.py:20
  10.6 14.9 %copy-start.6 = (f32[64,3,448]{0,2,1:T(8,128)}, f32[64,3,448]{0,2,1:T(8,128)S(1)}, u32[]{:S(2)}) copy-start(f32[64,3,448]{0,2,1:T(8,128)S(1)} %copy.174) | copy-start | bytes 1032196
  11.4 69.3 %collective-permute-start.2 = (bf16[64,3,192]{0,2,1:T(8,128)(2,1)}, bf16[64,3,192]{0,2,1:T(8,128)(2,1)S(1)}, u32[]{:S(2)}, u32[]{:S(2)}) collective-permute-start(bf16[64,3,192]{0,2,1:T(8,128)(2,1)} %get-tuple-element.25), channel_id=1, source_target_pairs={{0,2},{2,4},{4,6},{6,8},{8,10},{10,12},{12,14},{14,16},{16,18},{18... | collective-permute-start | bytes 221192 | tf_op jit(solution)/shard_map/ppermute | solution.py:17
  13.2 69.9 %collective-permute-start.3 = (bf16[64,3,192]{0,2,1:T(8,128)(2,1)S(1)}, bf16[64,3,192]{0,2,1:T(8,128)(2,1)S(1)}, u32[]{:S(2)}, u32[]{:S(2)}) collective-permute-start(bf16[64,3,192]{0,2,1:T(8,128)(2,1)S(1)} %get-tuple-element.26), channel_id=1, source_target_pairs={{2,0},{4,2},{6,4},{8,6},{10,8},{12,10},{14,12},{16,14},{18,16},{20... | collective-permute-start | bytes 221192 | tf_op jit(solution)/shard_map/ppermute | solution.py:20
  26.4 173.0 %copy-start.39 = (s32[64,14]{1,0:T(8,128)}, s32[64,14]{1,0:T(8,128)S(1)}, u32[]{:S(2)}) copy-start(s32[64,14]{1,0:T(8,128)S(1)} %copy.193) | copy-start | bytes 10756
  26.5 180.3 %copy-start.37 = (s32[64,14]{1,0:T(8,128)}, s32[64,14]{1,0:T(8,128)S(1)}, u32[]{:S(2)}) copy-start(s32[64,14]{1,0:T(8,128)S(1)} %copy.188) | copy-start | bytes 10756
  26.6 187.4 %copy-start.35 = (s32[64,14]{1,0:T(8,128)}, s32[64,14]{1,0:T(8,128)S(1)}, u32[]{:S(2)}) copy-start(s32[64,14]{1,0:T(8,128)S(1)} %copy.183) | copy-start | bytes 10756
  26.7 194.3 %copy-start.33 = (s32[64,14]{1,0:T(8,128)}, s32[64,14]{1,0:T(8,128)S(1)}, u32[]{:S(2)}) copy-start(s32[64,14]{1,0:T(8,128)S(1)} %copy.178) | copy-start | bytes 10756
  26.8 201.3 %copy-start.31 = (s32[64,14]{1,0:T(8,128)}, s32[64,14]{1,0:T(8,128)S(1)}, u32[]{:S(2)}) copy-start(s32[64,14]{1,0:T(8,128)S(1)} %copy.171) | copy-start | bytes 10756
  327.3 17.5 %copy-start.40 = (s32[64,14]{1,0:T(8,128)S(1)}, s32[64,14]{1,0:T(8,128)}, u32[]{:S(2)}) copy-start(s32[64,14]{1,0:T(8,128)} %copy-done.39) | copy-start | bytes 10756
  363.8 17.6 %copy-start.38 = (s32[64,14]{1,0:T(8,128)S(1)}, s32[64,14]{1,0:T(8,128)}, u32[]{:S(2)}) copy-start(s32[64,14]{1,0:T(8,128)} %copy-done.37) | copy-start | bytes 10756
  400.4 17.5 %copy-start.36 = (s32[64,14]{1,0:T(8,128)S(1)}, s32[64,14]{1,0:T(8,128)}, u32[]{:S(2)}) copy-start(s32[64,14]{1,0:T(8,128)} %copy-done.35) | copy-start | bytes 10756
  436.7 17.5 %copy-start.34 = (s32[64,14]{1,0:T(8,128)S(1)}, s32[64,14]{1,0:T(8,128)}, u32[]{:S(2)}) copy-start(s32[64,14]{1,0:T(8,128)} %copy-done.33) | copy-start | bytes 10756
  473.1 17.7 %copy-start.32 = (s32[64,14]{1,0:T(8,128)S(1)}, s32[64,14]{1,0:T(8,128)}, u32[]{:S(2)}) copy-start(s32[64,14]{1,0:T(8,128)} %copy-done.31) | copy-start | bytes 10756
  509.7 17.7 %copy-start.16 = (f32[64,14,32]{2,1,0:T(8,128)S(1)}, f32[64,14,32]{2,1,0:T(8,128)}, u32[]{:S(2)}) copy-start(f32[64,14,32]{2,1,0:T(8,128)} %get-tuple-element.56) | copy-start | bytes 344068
  509.7 17.7 %copy-start.52 = (f32[128]{0:T(128)S(1)}, f32[128]{0:T(128)}, u32[]{:S(2)}) copy-start(f32[128]{0:T(128)} %get-tuple-element.35) | copy-start | bytes 1540
  509.7 17.7 %copy-start.53 = (f32[128]{0:T(128)S(1)}, f32[128]{0:T(128)}, u32[]{:S(2)}) copy-start(f32[128]{0:T(128)} %get-tuple-element.36) | copy-start | bytes 1540
  509.7 17.7 %copy-start.54 = (f32[128]{0:T(128)S(1)}, f32[128]{0:T(128)}, u32[]{:S(2)}) copy-start(f32[128]{0:T(128)} %get-tuple-element.37) | copy-start | bytes 1540
  509.7 38.4 %slice-start = ((s8[14680064]{0:T(1024)(128)(4,1)}), s8[2097152]{0:T(1024)(128)(4,1)S(1)}, s32[]{:S(2)}) async-start(s8[14680064]{0:T(1024)(128)(4,1)} %bitcast.229), calls=%async_computation.2 | async-start | bytes 4194304
  527.4 20.8 %slice-start.1 = ((s8[14680064]{0:T(1024)(128)(4,1)}), s8[4194304]{0:T(1024)(128)(4,1)S(1)}, s32[]{:S(2)}) async-start(s8[14680064]{0:T(1024)(128)(4,1)} %bitcast.229), calls=%async_computation.3 | async-start | bytes 8388608
  527.4 20.8 %slice-start.2 = ((s8[14680064]{0:T(1024)(128)(4,1)}), s8[4194304]{0:T(1024)(128)(4,1)S(1)}, s32[]{:S(2)}) async-start(s8[14680064]{0:T(1024)(128)(4,1)} %bitcast.229), calls=%async_computation.4 | async-start | bytes 8388608
  527.4 20.8 %slice-start.3 = ((s8[14680064]{0:T(1024)(128)(4,1)}), s8[4194304]{0:T(1024)(128)(4,1)S(1)}, s32[]{:S(2)}) async-start(s8[14680064]{0:T(1024)(128)(4,1)} %bitcast.229), calls=%async_computation.5 | async-start | bytes 8388608
  527.4 20.8 %copy-start.18 = (f32[64,14,32]{2,1,0:T(8,128)S(1)}, f32[64,14,32]{2,1,0:T(8,128)}, u32[]{:S(2)}) copy-start(f32[64,14,32]{2,1,0:T(8,128)} %get-tuple-element.54) | copy-start | bytes 344068
  527.4 37.4 %slice-start.4 = ((s8[14680064]{0:T(1024)(128)(4,1)}), s8[4194304]{0:T(1024)(128)(4,1)S(1)}, s32[]{:S(2)}) async-start(s8[14680064]{0:T(1024)(128)(4,1)} %bitcast.242), calls=%async_computation.6 | async-start | bytes 8388608
  527.4 37.4 %slice-start.5 = ((s8[14680064]{0:T(1024)(128)(4,1)}), s8[4194304]{0:T(1024)(128)(4,1)S(1)}, s32[]{:S(2)}) async-start(s8[14680064]{0:T(1024)(128)(4,1)} %bitcast.242), calls=%async_computation.7 | async-start | bytes 8388608
  548.2 16.7 %slice-start.6 = ((s8[14680064]{0:T(1024)(128)(4,1)}), s8[4194304]{0:T(1024)(128)(4,1)S(1)}, s32[]{:S(2)}) async-start(s8[14680064]{0:T(1024)(128)(4,1)} %bitcast.242), calls=%async_computation.8 | async-start | bytes 8388608
  548.2 16.6 %slice-start.7 = ((s8[14680064]{0:T(1024)(128)(4,1)}), s8[2097152]{0:T(1024)(128)(4,1)S(1)}, s32[]{:S(2)}) async-start(s8[14680064]{0:T(1024)(128)(4,1)} %bitcast.242), calls=%async_computation.9 | async-start | bytes 4194304
  548.2 16.6 %copy-start.20 = (f32[64,14,32]{2,1,0:T(8,128)S(1)}, f32[64,14,32]{2,1,0:T(8,128)}, u32[]{:S(2)}) copy-start(f32[64,14,32]{2,1,0:T(8,128)} %get-tuple-element.52) | copy-start | bytes 344068
  564.9 10.9 %copy-start.22 = (f32[64,14,32]{2,1,0:T(8,128)S(1)}, f32[64,14,32]{2,1,0:T(8,128)}, u32[]{:S(2)}) copy-start(f32[64,14,32]{2,1,0:T(8,128)} %get-tuple-element.50) | copy-start | bytes 344068
  575.8 17.9 %copy-start.4 = (f32[64,14,32,128]{3,2,1,0:T(8,128)S(1)}, f32[64,14,32,128]{3,2,1,0:T(8,128)}, u32[]{:S(2)}) copy-start(f32[64,14,32,128]{3,2,1,0:T(8,128)} %reshape.367) | copy-start | bytes 44040196
  575.8 17.9 %copy-start.24 = (f32[64,14,32]{2,1,0:T(8,128)S(1)}, f32[64,14,32]{2,1,0:T(8,128)}, u32[]{:S(2)}) copy-start(f32[64,14,32]{2,1,0:T(8,128)} %get-tuple-element.48) | copy-start | bytes 344068
  593.6 10.9 %copy-start.26 = (f32[64,14,32]{2,1,0:T(8,128)S(1)}, f32[64,14,32]{2,1,0:T(8,128)}, u32[]{:S(2)}) copy-start(f32[64,14,32]{2,1,0:T(8,128)} %get-tuple-element.46) | copy-start | bytes 344068
  604.5 17.9 %copy-start.5 = (f32[64,14,32,128]{3,2,1,0:T(8,128)S(1)}, f32[64,14,32,128]{3,2,1,0:T(8,128)}, u32[]{:S(2)}) copy-start(f32[64,14,32,128]{3,2,1,0:T(8,128)} %reshape.365) | copy-start | bytes 44040196
  604.5 17.9 %copy-start.28 = (f32[64,14,32]{2,1,0:T(8,128)S(1)}, f32[64,14,32]{2,1,0:T(8,128)}, u32[]{:S(2)}) copy-start(f32[64,14,32]{2,1,0:T(8,128)} %get-tuple-element.44) | copy-start | bytes 344068
  622.4 10.9 %copy-start.30 = (f32[64,14,32]{2,1,0:T(8,128)S(1)}, f32[64,14,32]{2,1,0:T(8,128)}, u32[]{:S(2)}) copy-start(f32[64,14,32]{2,1,0:T(8,128)} %get-tuple-element.42) | copy-start | bytes 344068
  696.8 54.5 %all-to-all-start = ((bf16[64,448,128]{2,0,1:T(8,128)(2,1)}), bf16[64,448,128]{2,0,1:T(8,128)(2,1)}, u32[]{:S(2)}, u32[]{:S(2)}) async-start(bf16[64,448,128]{2,0,1:T(8,128)(2,1)} %copy.213), calls=%async_computation | async-start | bytes 14680064 | tf_op jit(solution)/shard_map/all_to_all | solution.py:144
  873.3 14.4 %copy-start.51 = (f32[2,128]{1,0:T(2,128)S(1)}, f32[2,128]{1,0:T(2,128)}, u32[]{:S(2)}) copy-start(f32[2,128]{1,0:T(2,128)} %param.21) | copy-start | bytes 3076
  873.3 14.5 %copy-start.49 = (bf16[256,128]{1,0:T(8,128)(2,1)S(1)}, bf16[256,128]{1,0:T(8,128)(2,1)}, u32[]{:S(2)}) copy-start(bf16[256,128]{1,0:T(8,128)(2,1)} %param.19) | copy-start | bytes 196612
  881.1 55.6 %all-to-all-start.1 = ((bf16[128,224,128]{2,1,0:T(8,128)(2,1)}), bf16[128,224,128]{2,1,0:T(8,128)(2,1)}, u32[]{:S(2)}, u32[]{:S(2)}) async-start(bf16[128,224,128]{2,1,0:T(8,128)(2,1)} %bitcast.241), calls=%async_computation.1 | async-start | bytes 14680064 | tf_op jit(solution)/shard_map/all_to_all | solution.py:146
  887.8 12.9 %copy-start.29 = (f32[64,14,32]{2,1,0:T(8,128)S(1)}, f32[64,14,32]{2,1,0:T(8,128)}, u32[]{:S(2)}) copy-start(f32[64,14,32]{2,1,0:T(8,128)} %get-tuple-element.44) | copy-start | bytes 344068
  887.8 12.9 %copy-start.45 = (f32[64,14,32]{2,1,0:T(8,128)S(1)}, f32[64,14,32]{2,1,0:T(8,128)}, u32[]{:S(2)}) copy-start(f32[64,14,32]{2,1,0:T(8,128)} %get-tuple-element.10) | copy-start | bytes 344068
  887.8 12.9 %copy-start.46 = (f32[64,14,32]{2,1,0:T(8,128)S(1)}, f32[64,14,32]{2,1,0:T(8,128)}, u32[]{:S(2)}) copy-start(f32[64,14,32]{2,1,0:T(8,128)} %get-tuple-element.11) | copy-start | bytes 344068
  887.8 14.1 %copy-start.25 = (f32[64,14,32]{2,1,0:T(8,128)S(1)}, f32[64,14,32]{2,1,0:T(8,128)}, u32[]{:S(2)}) copy-start(f32[64,14,32]{2,1,0:T(8,128)} %get-tuple-element.48) | copy-start | bytes 344068
  887.8 14.1 %copy-start.27 = (f32[64,14,32]{2,1,0:T(8,128)S(1)}, f32[64,14,32]{2,1,0:T(8,128)}, u32[]{:S(2)}) copy-start(f32[64,14,32]{2,1,0:T(8,128)} %get-tuple-element.46) | copy-start | bytes 344068
  887.8 14.1 %copy-start.43 = (f32[64,14,32]{2,1,0:T(8,128)S(1)}, f32[64,14,32]{2,1,0:T(8,128)}, u32[]{:S(2)}) copy-start(f32[64,14,32]{2,1,0:T(8,128)} %get-tuple-element.12) | copy-start | bytes 344068
  887.8 14.1 %copy-start.44 = (f32[64,14,32]{2,1,0:T(8,128)S(1)}, f32[64,14,32]{2,1,0:T(8,128)}, u32[]{:S(2)}) copy-start(f32[64,14,32]{2,1,0:T(8,128)} %get-tuple-element.13) | copy-start | bytes 344068
  887.8 15.5 %copy-start.21 = (f32[64,14,32]{2,1,0:T(8,128)S(1)}, f32[64,14,32]{2,1,0:T(8,128)}, u32[]{:S(2)}) copy-start(f32[64,14,32]{2,1,0:T(8,128)} %get-tuple-element.52) | copy-start | bytes 344068
  887.8 15.5 %copy-start.23 = (f32[64,14,32]{2,1,0:T(8,128)S(1)}, f32[64,14,32]{2,1,0:T(8,128)}, u32[]{:S(2)}) copy-start(f32[64,14,32]{2,1,0:T(8,128)} %get-tuple-element.50) | copy-start | bytes 344068
  887.8 15.5 %copy-start.41 = (f32[64,14,32]{2,1,0:T(8,128)S(1)}, f32[64,14,32]{2,1,0:T(8,128)}, u32[]{:S(2)}) copy-start(f32[64,14,32]{2,1,0:T(8,128)} %get-tuple-element.14) | copy-start | bytes 344068
  887.9 15.5 %copy-start.42 = (f32[64,14,32]{2,1,0:T(8,128)S(1)}, f32[64,14,32]{2,1,0:T(8,128)}, u32[]{:S(2)}) copy-start(f32[64,14,32]{2,1,0:T(8,128)} %get-tuple-element.15) | copy-start | bytes 344068
  887.9 16.8 %copy-start.17 = (f32[64,14,32]{2,1,0:T(8,128)S(1)}, f32[64,14,32]{2,1,0:T(8,128)}, u32[]{:S(2)}) copy-start(f32[64,14,32]{2,1,0:T(8,128)} %get-tuple-element.56) | copy-start | bytes 344068
  887.9 16.8 %copy-start.19 = (f32[64,14,32]{2,1,0:T(8,128)S(1)}, f32[64,14,32]{2,1,0:T(8,128)}, u32[]{:S(2)}) copy-start(f32[64,14,32]{2,1,0:T(8,128)} %get-tuple-element.54) | copy-start | bytes 344068
  887.9 18.2 %copy-start.8 = (f32[64,3,14,32]{3,2,1,0:T(8,128)S(1)}, f32[64,3,14,32]{3,2,1,0:T(8,128)}, u32[]{:S(2)}) copy-start(f32[64,3,14,32]{3,2,1,0:T(8,128)} %get-tuple-element.57) | copy-start | bytes 1032196
  887.9 18.2 %copy-start.9 = (f32[64,3,14,32]{3,2,1,0:T(8,128)S(1)}, f32[64,3,14,32]{3,2,1,0:T(8,128)}, u32[]{:S(2)}) copy-start(f32[64,3,14,32]{3,2,1,0:T(8,128)} %get-tuple-element.55) | copy-start | bytes 1032196
  887.9 18.1 %copy-start.10 = (f32[64,3,14,32]{3,2,1,0:T(8,128)S(1)}, f32[64,3,14,32]{3,2,1,0:T(8,128)}, u32[]{:S(2)}) copy-start(f32[64,3,14,32]{3,2,1,0:T(8,128)} %get-tuple-element.53) | copy-start | bytes 1032196
  887.9 18.1 %copy-start.11 = (f32[64,3,14,32]{3,2,1,0:T(8,128)S(1)}, f32[64,3,14,32]{3,2,1,0:T(8,128)}, u32[]{:S(2)}) copy-start(f32[64,3,14,32]{3,2,1,0:T(8,128)} %get-tuple-element.51) | copy-start | bytes 1032196
  887.9 18.1 %copy-start.12 = (f32[64,3,14,32]{3,2,1,0:T(8,128)S(1)}, f32[64,3,14,32]{3,2,1,0:T(8,128)}, u32[]{:S(2)}) copy-start(f32[64,3,14,32]{3,2,1,0:T(8,128)} %get-tuple-element.49) | copy-start | bytes 1032196
  887.9 18.1 %copy-start.13 = (f32[64,3,14,32]{3,2,1,0:T(8,128)S(1)}, f32[64,3,14,32]{3,2,1,0:T(8,128)}, u32[]{:S(2)}) copy-start(f32[64,3,14,32]{3,2,1,0:T(8,128)} %get-tuple-element.47) | copy-start | bytes 1032196
  887.9 18.1 %copy-start.14 = (f32[64,3,14,32]{3,2,1,0:T(8,128)S(1)}, f32[64,3,14,32]{3,2,1,0:T(8,128)}, u32[]{:S(2)}) copy-start(f32[64,3,14,32]{3,2,1,0:T(8,128)} %get-tuple-element.45) | copy-start | bytes 1032196
  888.0 18.1 %copy-start.15 = (f32[64,3,14,32]{3,2,1,0:T(8,128)S(1)}, f32[64,3,14,32]{3,2,1,0:T(8,128)}, u32[]{:S(2)}) copy-start(f32[64,3,14,32]{3,2,1,0:T(8,128)} %get-tuple-element.43) | copy-start | bytes 1032196
  906.1 37.7 %copy-start.55 = (bf16[128,128]{1,0:T(8,128)(2,1)S(1)}, bf16[128,128]{1,0:T(8,128)(2,1)}, u32[]{:S(2)}) copy-start(bf16[128,128]{1,0:T(8,128)(2,1)} %param.20) | copy-start | bytes 98308
  (7 other events, 52.8 us)
where the time goes:
time: 967 us; the launch traced here: 959 us
  matrix products  533 us (55%)
  local copies, waits for them, and re-layouts  231 us (24%)
  waiting for transfers between devices  129 us (13%)
  other arithmetic  46.4 us (5%)
  starting transfers between devices  18.9 us (2%)
    dot_general x8, matrix products, edge_pass(): jnp.dot(hidden.reshape(-1, feat_width), edge_out, preferred_element_type=...  158 us
    dot_general x8, matrix products, edge_pass(): jnp.einsum('fbc,fcx->fbx', select_bf, dst_low, preferred_element_type=jnp...  151 us
    reshape x8, local copies, waits for them, and re-layouts, edge_pass(): near_dst = near_dst.reshape(own_src.shape)  141 us
    dot_general x8, matrix products, edge_pass(): jnp.einsum('fbc,fcx->fbx', select_bf, dst_high, preferred_element_type=jn...  57.1 us
    ppermute x2, waiting for transfers between devices, with_halo(): lax.ppermute(lax.slice_in_dim(block, block.shape[dim] - width, None, axis...  53.9 us
    all_to_all x1, waiting for transfers between devices, shards(): lax.all_to_all(mean_msg, 'tm', split_axis=1, concat_axis=0, tiled=True)  47.5 us
    convert_element_type x1, other arithmetic, split_parts(): low_part = (values - high_part.astype(jnp.float32)).astype(jnp.bfloat16)  29.6 us
    another operation x1, local copies, waits for them, and re-layouts, edge_pass(): flat_dst = other_dst.reshape(frames, other_blocks, block_len * feat_width)  28.5 us
  transfers between devices with their start and end apart: 6, of which 4 were waited for; matrix products, arithmetic and copies ran while one was open for 6% of the time, Pallas kernels for 0%

commit v1 on v0

--- a/solution.py
+++ b/solution.py
@@ -141,7 +141,10 @@
     )
     mean_msg = (summed / slot_count).astype(jnp.bfloat16).reshape(frames, local_rows, feat_width)
     new_positions = positions + (moved / slot_count).reshape(frames, 3, local_rows)
-    regrouped = lax.all_to_all(mean_msg, "tm", split_axis=1, concat_axis=0, tiled=True)
+    regrouped = jnp.concatenate(
+        lax.all_to_all(jnp.stack(jnp.split(mean_msg, lax.axis_size("tm"), axis=1)), "tm", 0, 0),
+        axis=0,
+    )
     conv_all = spectral_conv(regrouped, spectral, regrouped.shape[0])
     conv_own = lax.all_to_all(conv_all, "tm", split_axis=0, concat_axis=1, tiled=True)
     node_pre = (

time: 967 us -> 956 us (0.989)
  local copies, waits for them, and re-layouts: 231 us -> 213 us
    reshape x1 -> x0, local copies, waits for them, and re-layouts: 10.8 us -> none  [shards(): (summed / slot_count).astype(jnp.bfloat16)]
    unnamed x136 -> x134, local copies, waits for them, and re-layouts: 23.7 us -> 20.7 us
where the time goes in v1:
time: 956 us; the launch traced here: 948 us
  matrix products  535 us (56%)
  local copies, waits for them, and re-layouts  213 us (22%)
  waiting for transfers between devices  129 us (13%)
  other arithmetic  50.3 us (5%)
  starting transfers between devices  19.1 us (2%)
    dot_general x8, matrix products, edge_pass(): jnp.dot(hidden.reshape(-1, feat_width), edge_out, preferred_element_type=...  158 us
    dot_general x8, matrix products, edge_pass(): jnp.einsum('fbc,fcx->fbx', select_bf, dst_low, preferred_element_type=jnp...  151 us
    reshape x8, local copies, waits for them, and re-layouts, edge_pass(): near_dst = near_dst.reshape(own_src.shape)  141 us
    dot_general x8, matrix products, edge_pass(): jnp.einsum('fbc,fcx->fbx', select_bf, dst_high, preferred_element_type=jn...  57 us
    ppermute x2, waiting for transfers between devices, with_halo(): lax.ppermute(lax.slice_in_dim(block, block.shape[dim] - width, None, axis...  53.9 us
    all_to_all x1, waiting for transfers between devices, shards(): lax.all_to_all(jnp.stack(jnp.split(mean_msg, lax.axis_size('tm'), axis=1)...  47.5 us
    convert_element_type x1, other arithmetic, split_parts(): low_part = (values - high_part.astype(jnp.float32)).astype(jnp.bfloat16)  29.6 us
    another operation x1, local copies, waits for them, and re-layouts, edge_pass(): flat_dst = other_dst.reshape(frames, other_blocks, block_len * feat_width)  28.5 us
  transfers between devices with their start and end apart: 6, of which 4 were waited for; matrix products, arithmetic and copies ran while one was open for 6% of the time, Pallas kernels for 0%

profile of v1, /device:TPU:1, one launch (start us, length us, event | category | flops | bytes accessed | tf_op | source)
XLA Modules:
  0.0 948.1 jit_solution(8848774892831387748)
XLA Ops:
  0.7 6.1 fusion.134
  6.7 2.6 collective-permute-start
  14.3 10.3 %fusion.99 = f32[64,448,128]{2,1,0:T(8,128)} fusion(bf16[64,448,128]{2,1,0:T(8,128)(2,1)} %param.11, bf16[256,128]{1,0:T(8,128)(2,1)S(1)} %copy-done.47), kind=kOutput, calls=%fused_computation.190 | convolution fusion | flops 939524096 | bytes 22052864 | tf_op jit(solution)/shard_map/dot_general | solution.py:131
  26.8 53.9 %collective-permute-done.2 = bf16[64,3,192]{0,2,1:T(8,128)(2,1)S(1)} collective-permute-done((bf16[64,3,192]{0,2,1:T(8,128)(2,1)}, bf16[64,3,192]{0,2,1:T(8,128)(2,1)S(1)}, u32[]{:S(2)}, u32[]{:S(2)}) %collective-permute-start.2) | collective-permute-done | bytes 73760 | tf_op jit(solution)/shard_map/ppermute | solution.py:17
  84.1 2.8 copy.78
  91.8 2.5 multiply_reduce_fusion.10
  96.7 2.5 multiply_reduce_fusion.12
  104.1 2.5 multiply_reduce_fusion.15
  106.6 13.9 %fusion.3 = f32[64,832,128]{2,1,0:T(8,128)} fusion(bf16[64,192,128]{2,1,0:T(8,128)(2,1)} %collective-permute-done.1, bf16[64,448,128]{2,1,0:T(8,128)(2,1)} %param.11, bf16[64,192,128]{2,1,0:T(8,128)(2,1)} %collective-permute-done, bf16[256,128]{1,0:T(8,128)(2,1)S(1)} %copy-done.47), kind=kOutput, calls=%fused_computation.37 | convolution fusion | flops 1785724928 | bytes 40927232 | tf_op jit(solution)/shard_map/dot_general | solution.py:136
  120.5 28.5 %reshape_reshape.6 = f32[64,26,4096]{2,1,0:T(8,128)} reshape(f32[64,832,128]{2,1,0:T(8,128)} %fusion.3) | data formatting | bytes 54525952 | tf_op jit(solution)/shard_map/reshape;reshape | solution.py:34
  148.9 29.6 %subtract_convert_fusion = (bf16[64,26,4096]{2,1,0:T(8,128)(2,1)}, bf16[64,26,4096]{2,1,0:T(8,128)(2,1)S(1)}) fusion(f32[64,26,4096]{2,1,0:T(8,128)} %reshape_reshape.6), kind=kLoop, calls=%fused_computation.5 | loop fusion | flops 27262976 | bytes 54525952 | tf_op jit(solution)/shard_map/convert_element_type | solution.py:27
  178.5 7.1 fusion.52
  185.6 7.1 fusion.51
  192.7 7.1 fusion.50
  199.8 7.4 fusion.49
  207.1 7.2 fusion.48
  214.3 7.1 fusion.47
  221.4 7.1 fusion.46
  228.5 7.1 fusion.45
  235.6 18.9 %convolution_add_fusion.3 = f32[64,14,4096]{2,1,0:T(8,128)} fusion(f32[64,14,4096]{2,1,0:T(8,128)} %fusion.52, bf16[64,26,4096]{2,1,0:T(8,128)(2,1)} %get-tuple-element.14, s32[64,14]{1,0:T(8,128)S(1)} %copy.110), kind=kOutput, calls=%fused_computation.47 | convolution fusion | flops 194580736 | bytes 42995200 | tf_op jit(solution)/shard_map/fbc,fcx->fbx/dot_general | solution.py:45
  254.5 17.7 %reshape.366 = f32[64,14,32,128]{3,2,1,0:T(8,128)} reshape(f32[64,14,4096]{2,1,0:T(8,128)} %convolution_add_fusion.3) | data formatting | bytes 29360128 | tf_op jit(solution)/shard_map/reshape | solution.py:46
  272.2 18.9 %convolution_add_fusion.4 = f32[64,14,4096]{2,1,0:T(8,128)} fusion(f32[64,14,4096]{2,1,0:T(8,128)} %fusion.51, bf16[64,26,4096]{2,1,0:T(8,128)(2,1)} %get-tuple-element.14, s32[64,14]{1,0:T(8,128)S(1)} %copy.105), kind=kOutput, calls=%fused_computation.48 | convolution fusion | flops 194580736 | bytes 42995200 | tf_op jit(solution)/shard_map/fbc,fcx->fbx/dot_general | solution.py:45
  291.1 17.5 %reshape.365 = f32[64,14,32,128]{3,2,1,0:T(8,128)} reshape(f32[64,14,4096]{2,1,0:T(8,128)} %convolution_add_fusion.4) | data formatting | bytes 29360128 | tf_op jit(solution)/shard_map/reshape | solution.py:46
  308.5 18.9 %convolution_add_fusion.5 = f32[64,14,4096]{2,1,0:T(8,128)} fusion(f32[64,14,4096]{2,1,0:T(8,128)} %fusion.50, bf16[64,26,4096]{2,1,0:T(8,128)(2,1)} %get-tuple-element.14, s32[64,14]{1,0:T(8,128)S(1)} %copy.100), kind=kOutput, calls=%fused_computation.49 | convolution fusion | flops 194580736 | bytes 42995200 | tf_op jit(solution)/shard_map/fbc,fcx->fbx/dot_general | solution.py:45
  327.4 17.5 %reshape.364 = f32[64,14,32,128]{3,2,1,0:T(8,128)} reshape(f32[64,14,4096]{2,1,0:T(8,128)} %convolution_add_fusion.5) | data formatting | bytes 29360128 | tf_op jit(solution)/shard_map/reshape | solution.py:46
  344.9 19.0 %convolution_add_fusion.6 = f32[64,14,4096]{2,1,0:T(8,128)} fusion(f32[64,14,4096]{2,1,0:T(8,128)} %fusion.49, bf16[64,26,4096]{2,1,0:T(8,128)(2,1)} %get-tuple-element.14, s32[64,14]{1,0:T(8,128)S(1)} %copy-done.39), kind=kOutput, calls=%fused_computation.50 | convolution fusion | flops 194580736 | bytes 42995200 | tf_op jit(solution)/shard_map/fbc,fcx->fbx/dot_general | solution.py:45
  363.9 17.8 %reshape.363 = f32[64,14,32,128]{3,2,1,0:T(8,128)} reshape(f32[64,14,4096]{2,1,0:T(8,128)} %convolution_add_fusion.6) | data formatting | bytes 29360128 | tf_op jit(solution)/shard_map/reshape | solution.py:46
  381.7 19.0 %convolution_add_fusion.7 = f32[64,14,4096]{2,1,0:T(8,128)} fusion(f32[64,14,4096]{2,1,0:T(8,128)} %fusion.48, bf16[64,26,4096]{2,1,0:T(8,128)(2,1)} %get-tuple-element.14, s32[64,14]{1,0:T(8,128)S(1)} %copy-done.37), kind=kOutput, calls=%fused_computation.51 | convolution fusion | flops 194580736 | bytes 42995200 | tf_op jit(solution)/shard_map/fbc,fcx->fbx/dot_general | solution.py:45
  400.7 17.5 %reshape.362 = f32[64,14,32,128]{3,2,1,0:T(8,128)} reshape(f32[64,14,4096]{2,1,0:T(8,128)} %convolution_add_fusion.7) | data formatting | bytes 29360128 | tf_op jit(solution)/shard_map/reshape | solution.py:46
  418.2 18.9 %convolution_add_fusion.8 = f32[64,14,4096]{2,1,0:T(8,128)} fusion(f32[64,14,4096]{2,1,0:T(8,128)} %fusion.47, bf16[64,26,4096]{2,1,0:T(8,128)(2,1)} %get-tuple-element.14, s32[64,14]{1,0:T(8,128)S(1)} %copy-done.35), kind=kOutput, calls=%fused_computation.52 | convolution fusion | flops 194580736 | bytes 42995200 | tf_op jit(solution)/shard_map/fbc,fcx->fbx/dot_general | solution.py:45
  437.1 17.5 %reshape.361 = f32[64,14,32,128]{3,2,1,0:T(8,128)} reshape(f32[64,14,4096]{2,1,0:T(8,128)} %convolution_add_fusion.8) | data formatting | bytes 29360128 | tf_op jit(solution)/shard_map/reshape | solution.py:46
  454.6 18.9 %convolution_add_fusion.9 = f32[64,14,4096]{2,1,0:T(8,128)} fusion(f32[64,14,4096]{2,1,0:T(8,128)} %fusion.46, bf16[64,26,4096]{2,1,0:T(8,128)(2,1)} %get-tuple-element.14, s32[64,14]{1,0:T(8,128)S(1)} %copy-done.33), kind=kOutput, calls=%fused_computation.53 | convolution fusion | flops 194580736 | bytes 42995200 | tf_op jit(solution)/shard_map/fbc,fcx->fbx/dot_general | solution.py:45
  473.5 17.6 %reshape.360 = f32[64,14,32,128]{3,2,1,0:T(8,128)} reshape(f32[64,14,4096]{2,1,0:T(8,128)} %convolution_add_fusion.9) | data formatting | bytes 29360128 | tf_op jit(solution)/shard_map/reshape | solution.py:46
  491.1 18.9 %convolution_add_fusion.10 = f32[64,14,4096]{2,1,0:T(8,128)} fusion(f32[64,14,4096]{2,1,0:T(8,128)} %fusion.45, bf16[64,26,4096]{2,1,0:T(8,128)(2,1)} %get-tuple-element.14, s32[64,14]{1,0:T(8,128)S(1)} %copy-done.31), kind=kOutput, calls=%fused_computation.54 | convolution fusion | flops 194580736 | bytes 42995200 | tf_op jit(solution)/shard_map/fbc,fcx->fbx/dot_general | solution.py:45
  510.1 17.6 %reshape.359 = f32[64,14,32,128]{3,2,1,0:T(8,128)} reshape(f32[64,14,4096]{2,1,0:T(8,128)} %convolution_add_fusion.10) | data formatting | bytes 29360128 | tf_op jit(solution)/shard_map/reshape | solution.py:46
  527.8 20.7 %divide_multiply_fusion = f32[64,14,32,128]{3,2,1,0:T(8,128)} fusion(f32[128]{0:T(128)S(1)} %copy-done.52, f32[64,14,32,128]{3,2,1,0:T(8,128)} %bitcast.226, f32[64,14,32,128]{3,2,1,0:T(8,128)} %reshape.366, f32[64,14,32]{2,1,0:T(8,128)S(1)} %copy-done.15, f32[128]{0:T(128)S(1)} %copy-done.53, f32[128]{0:T(128)S(1)} %copy-done.51, ...), kind=kOutput, calls=%fused_computation.21 | convolution fusion | flops 990904320 | bytes 44189184 | tf_op jit(solution)/shard_map/dot_general | solution.py:55
  548.5 16.6 %divide_multiply_fusion.1 = f32[64,14,32,128]{3,2,1,0:T(8,128)} fusion(f32[128]{0:T(128)S(1)} %copy-done.52, f32[64,14,32,128]{3,2,1,0:T(8,128)S(1)} %bitcast.230, f32[64,14,32,128]{3,2,1,0:T(8,128)} %reshape.365, f32[64,14,32]{2,1,0:T(8,128)S(1)} %copy-done.17, f32[128]{0:T(128)S(1)} %copy-done.53, f32[128]{0:T(128)S(1)} %copy-done.51, ...), kind=kOutput, calls=%fused_computation.23 | convolution fusion | flops 990904320 | bytes 44189184 | tf_op jit(solution)/shard_map/dot_general | solution.py:55
  565.2 10.9 %divide_multiply_fusion.2 = f32[64,14,32,128]{3,2,1,0:T(8,128)} fusion(f32[128]{0:T(128)S(1)} %copy-done.52, f32[64,14,32,128]{3,2,1,0:T(8,128)S(1)} %bitcast.231, f32[64,14,32,128]{3,2,1,0:T(8,128)S(1)} %bitcast.242, f32[64,14,32]{2,1,0:T(8,128)S(1)} %copy-done.19, f32[128]{0:T(128)S(1)} %copy-done.53, f32[128]{0:T(128)S(1)} %copy-done.51, ...), kind=kOutput, calls=%fused_computation.25 | convolution fusion | flops 990904320 | bytes 44189184 | tf_op jit(solution)/shard_map/dot_general | solution.py:55
  576.1 17.8 %divide_multiply_fusion.3 = f32[64,14,32,128]{3,2,1,0:T(8,128)} fusion(f32[128]{0:T(128)S(1)} %copy-done.52, f32[64,14,32,128]{3,2,1,0:T(8,128)S(1)} %bitcast.232, f32[64,14,32,128]{3,2,1,0:T(8,128)} %reshape.363, f32[64,14,32]{2,1,0:T(8,128)S(1)} %copy-done.21, f32[128]{0:T(128)S(1)} %copy-done.53, f32[128]{0:T(128)S(1)} %copy-done.51, ...), kind=kOutput, calls=%fused_computation.27 | convolution fusion | flops 990904320 | bytes 44189184 | tf_op jit(solution)/shard_map/dot_general | solution.py:55
  594.0 10.9 %divide_multiply_fusion.4 = f32[64,14,32,128]{3,2,1,0:T(8,128)} fusion(f32[128]{0:T(128)S(1)} %copy-done.52, f32[64,14,32,128]{3,2,1,0:T(8,128)S(1)} %bitcast.233, f32[64,14,32,128]{3,2,1,0:T(8,128)S(1)} %copy-done.3, f32[64,14,32]{2,1,0:T(8,128)S(1)} %copy-done.23, f32[128]{0:T(128)S(1)} %copy-done.53, f32[128]{0:T(128)S(1)} %copy-done.51, ...), kind=kOutput, calls=%fused_computation.29 | convolution fusion | flops 990904320 | bytes 44189184 | tf_op jit(solution)/shard_map/dot_general | solution.py:55
  604.8 17.8 %divide_multiply_fusion.5 = f32[64,14,32,128]{3,2,1,0:T(8,128)} fusion(f32[128]{0:T(128)S(1)} %copy-done.52, f32[64,14,32,128]{3,2,1,0:T(8,128)S(1)} %bitcast.234, f32[64,14,32,128]{3,2,1,0:T(8,128)} %reshape.361, f32[64,14,32]{2,1,0:T(8,128)S(1)} %copy-done.25, f32[128]{0:T(128)S(1)} %copy-done.53, f32[128]{0:T(128)S(1)} %copy-done.51, ...), kind=kOutput, calls=%fused_computation.31 | convolution fusion | flops 990904320 | bytes 44189184 | tf_op jit(solution)/shard_map/dot_general | solution.py:55
  622.7 10.9 %divide_multiply_fusion.6 = f32[64,14,32,128]{3,2,1,0:T(8,128)} fusion(f32[128]{0:T(128)S(1)} %copy-done.52, f32[64,14,32,128]{3,2,1,0:T(8,128)S(1)} %bitcast.235, f32[64,14,32,128]{3,2,1,0:T(8,128)S(1)} %copy-done.4, f32[64,14,32]{2,1,0:T(8,128)S(1)} %copy-done.27, f32[128]{0:T(128)S(1)} %copy-done.53, f32[128]{0:T(128)S(1)} %copy-done.51, ...), kind=kOutput, calls=%fused_computation.33 | convolution fusion | flops 990904320 | bytes 44189184 | tf_op jit(solution)/shard_map/dot_general | solution.py:55
  633.6 52.5 %multiply_reduce_fusion.7 = (f32[64,14,32]{2,1,0:T(8,128)}, f32[64,14,32]{2,1,0:T(8,128)}, f32[64,14,32]{2,1,0:T(8,128)}, f32[64,14,32]{2,1,0:T(8,128)}, f32[64,...) fusion(f32[128]{0:T(128)S(1)} %copy-done.55, ...), kind=kOutput, calls=%fused_computation.17 | convolution fusion | flops 1082425344 | bytes 140527616 | tf_op jit(solution)/shard_map/dot_general | solution.py:55
  686.1 3.6 slice_bitcast_fusion.3
  689.7 3.7 pad_maximum_fusion.1
  693.4 7.0 all-to-all-start
  700.7 47.5 %all-to-all-done = bf16[2,64,224,128]{3,2,1,0:T(8,128)(2,1)} async-done(((bf16[2,64,224,128]{3,2,1,0:T(8,128)(2,1)}), bf16[2,64,224,128]{3,2,1,0:T(8,128)(2,1)}, u32[]{:S(2)}, u32[]{:S(2)}) %all-to-all-start) | async-done | bytes 7340064 | tf_op jit(solution)/shard_map/all_to_all | solution.py:145
  748.2 11.2 %fusion.11 = f32[128,28672]{1,0:T(8,128)} fusion(bf16[16,8,224,128]{3,2,1,0:T(8,128)(2,1)} %bitcast.67, f32[64,128]{1,0:T(8,128)S(1)} %get-tuple-element.64, f32[64,128]{1,0:T(8,128)S(1)} %get-tuple-element.65), kind=kOutput, calls=%fused_computation.44 | convolution fusion | flops 939589632 | bytes 22085632 | tf_op jit(solution)/shard_map/dot_general | solution.py:77
  759.4 13.6 %fusion = bf16[128,28672]{1,0:T(8,128)(2,1)} fusion(f32[128,28672]{1,0:T(8,128)} %fusion.11, bf16[16,8,224,128]{3,2,1,0:T(8,128)(2,1)} %bitcast.67, f32[64,128]{1,0:T(8,128)S(1)} %get-tuple-element.64, f32[64,128]{1,0:T(8,128)S(1)} %get-tuple-element.65), kind=kOutput, calls=%fused_computation.3 | convolution fusion | flops 946946048 | bytes 29425664 | tf_op jit(solution)/shard_map/dot_general | solution.py:77
  773.0 3.8 slice_bitcast_fusion
  780.5 4.0 convolution_subtract_fusion
  784.5 4.2 convolution_add_fusion.11
  788.7 6.7 pad_maximum_fusion
  795.4 5.2 copy-done.1
  800.6 14.5 %fusion.15 = f32[128,28672]{1,0:T(8,128)} fusion(f32[16,8,224,128]{3,2,1,0:T(8,128)S(1)} %bitcast.223, f32[128,64]{0,1:T(8,128)S(1)} %get-tuple-element.39, f32[128,64]{0,1:T(8,128)S(1)} %get-tuple-element.38), kind=kOutput, calls=%fused_computation.57 | convolution fusion | flops 939589632 | bytes 29425664 | tf_op jit(solution)/shard_map/dot_general | solution.py:99
  815.1 24.5 %convolution_add_fusion.1 = f32[128,28672]{1,0:T(8,128)} fusion(f32[128,28672]{1,0:T(8,128)} %fusion.15, f32[16,8,224,128]{3,2,1,0:T(8,128)} %bitcast.224, f32[128,64]{0,1:T(8,128)S(1)} %get-tuple-element.39, f32[128,64]{0,1:T(8,128)S(1)} %get-tuple-element.38), kind=kOutput, calls=%fused_computation.1 | convolution fusion | flops 943276032 | bytes 44105728 | tf_op jit(solution)/shard_map/dot_general | solution.py:100
  839.6 22.9 %fusion.16 = bf16[16,8,224,128]{3,1,2,0:T(8,128)(2,1)} fusion(f32[128,28672]{1,0:T(8,128)} %convolution_add_fusion.1, f32[16,8,224,128]{3,2,1,0:T(8,128)} %bitcast.225, f32[128,64]{0,1:T(8,128)S(1)} %get-tuple-element.39, f32[128,64]{0,1:T(8,128)S(1)} %get-tuple-element.38), kind=kOutput, calls=%fused_computation.58 | convolution fusion | flops 961609728 | bytes 36765696 | tf_op jit(solution)/shard_map/dot_general | solution.py:101
  862.5 7.8 copy.140
  870.3 6.6 all-to-all-start.1
  877.2 12.7 %fusion.101 = f32[64,448,128]{2,1,0:T(8,128)} fusion(bf16[64,448,128]{2,1,0:T(8,128)(2,1)} %param.11, bf16[256,128]{1,0:T(8,128)(2,1)S(1)} %copy-done.48), kind=kOutput, calls=%fused_computation.192 | convolution fusion | flops 939524096 | bytes 22052864 | tf_op jit(solution)/shard_map/dot_general | solution.py:151
  895.3 3.6 add_multiply_fusion
  900.6 25.3 %all-to-all-done.1 = bf16[128,224,128]{2,1,0:T(8,128)(2,1)} async-done(((bf16[128,224,128]{2,1,0:T(8,128)(2,1)}), bf16[128,224,128]{2,1,0:T(8,128)(2,1)}, u32[]{:S(2)}, u32[]{:S(2)}) %all-to-all-start.1) | async-done | bytes 7340064 | tf_op jit(solution)/shard_map/all_to_all | solution.py:149
  925.9 7.2 copy.115
  933.1 14.8 %add_convert_fusion = bf16[64,448,128]{2,1,0:T(8,128)(2,1)} fusion(bf16[64,448,128]{2,1,0:T(8,128)(2,1)} %param.11, f32[128]{0:T(128)S(1)} %get-tuple-element.37, f32[64,448,128]{2,1,0:T(8,128)} %fusion.101, bf16[64,448,128]{2,1,0:T(8,128)(2,1)} %bitcast.245, f32[128]{0:T(128)S(1)} %get-tuple-element.36, bf16[128,128]{1,0:T(8,128)(2,1)S(1)} %copy-done.54, ...), kind=kOutput, calls=%fused_computation.18 | convolution fusion | flops 1919418368 | bytes 36766720 | tf_op jit(solution)/shard_map/dot_general | solution.py:158
  (171 shorter events, 33.8 us)
Async XLA Ops:
  0.6 527.0 %copy-start = (bf16[128,128]{1,0:T(8,128)(2,1)S(1)}, bf16[128,128]{1,0:T(8,128)(2,1)}, u32[]{:S(2)}) copy-start(bf16[128,128]{1,0:T(8,128)(2,1)} %param.15) | copy-start | bytes 98308
  0.6 13.7 %copy-start.47 = (bf16[256,128]{1,0:T(8,128)(2,1)S(1)}, bf16[256,128]{1,0:T(8,128)(2,1)}, u32[]{:S(2)}) copy-start(bf16[256,128]{1,0:T(8,128)(2,1)} %param.14) | copy-start | bytes 196612
  6.7 99.9 %collective-permute-start = (bf16[64,192,128]{2,1,0:T(8,128)(2,1)}, bf16[64,192,128]{2,1,0:T(8,128)(2,1)}, u32[]{:S(2)}, u32[]{:S(2)}) collective-permute-start(bf16[64,192,128]{2,1,0:T(8,128)(2,1)} %get-tuple-element.21), channel_id=1, source_target_pairs={{0,2},{2,4},{4,6},{6,8},{8,10},{10,12},{12,14},{14,16},{16,18},{18... | collective-permute-start | bytes 9437192 | tf_op jit(solution)/shard_map/ppermute | solution.py:17
  9.3 97.3 %collective-permute-start.1 = (bf16[64,192,128]{2,1,0:T(8,128)(2,1)}, bf16[64,192,128]{2,1,0:T(8,128)(2,1)}, u32[]{:S(2)}, u32[]{:S(2)}) collective-permute-start(bf16[64,192,128]{2,1,0:T(8,128)(2,1)} %get-tuple-element.22), channel_id=1, source_target_pairs={{2,0},{4,2},{6,4},{8,6},{10,8},{12,10},{14,12},{16,14},{18,16},{20... | collective-permute-start | bytes 9437192 | tf_op jit(solution)/shard_map/ppermute | solution.py:20
  10.6 14.8 %copy-start.5 = (f32[64,3,448]{0,2,1:T(8,128)}, f32[64,3,448]{0,2,1:T(8,128)S(1)}, u32[]{:S(2)}) copy-start(f32[64,3,448]{0,2,1:T(8,128)S(1)} %copy.76) | copy-start | bytes 1032196
  11.4 69.3 %collective-permute-start.2 = (bf16[64,3,192]{0,2,1:T(8,128)(2,1)}, bf16[64,3,192]{0,2,1:T(8,128)(2,1)S(1)}, u32[]{:S(2)}, u32[]{:S(2)}) collective-permute-start(bf16[64,3,192]{0,2,1:T(8,128)(2,1)} %get-tuple-element.23), channel_id=1, source_target_pairs={{0,2},{2,4},{4,6},{6,8},{8,10},{10,12},{12,14},{14,16},{16,18},{18... | collective-permute-start | bytes 221192 | tf_op jit(solution)/shard_map/ppermute | solution.py:17
  13.2 69.9 %collective-permute-start.3 = (bf16[64,3,192]{0,2,1:T(8,128)(2,1)S(1)}, bf16[64,3,192]{0,2,1:T(8,128)(2,1)S(1)}, u32[]{:S(2)}, u32[]{:S(2)}) collective-permute-start(bf16[64,3,192]{0,2,1:T(8,128)(2,1)S(1)} %get-tuple-element.24), channel_id=1, source_target_pairs={{2,0},{4,2},{6,4},{8,6},{10,8},{12,10},{14,12},{16,14},{18,16},{20... | collective-permute-start | bytes 221192 | tf_op jit(solution)/shard_map/ppermute | solution.py:20
  26.4 173.4 %copy-start.38 = (s32[64,14]{1,0:T(8,128)}, s32[64,14]{1,0:T(8,128)S(1)}, u32[]{:S(2)}) copy-start(s32[64,14]{1,0:T(8,128)S(1)} %copy.95) | copy-start | bytes 10756
  26.5 180.6 %copy-start.36 = (s32[64,14]{1,0:T(8,128)}, s32[64,14]{1,0:T(8,128)S(1)}, u32[]{:S(2)}) copy-start(s32[64,14]{1,0:T(8,128)S(1)} %copy.90) | copy-start | bytes 10756
  26.6 187.7 %copy-start.34 = (s32[64,14]{1,0:T(8,128)}, s32[64,14]{1,0:T(8,128)S(1)}, u32[]{:S(2)}) copy-start(s32[64,14]{1,0:T(8,128)S(1)} %copy.85) | copy-start | bytes 10756
  26.7 194.7 %copy-start.32 = (s32[64,14]{1,0:T(8,128)}, s32[64,14]{1,0:T(8,128)S(1)}, u32[]{:S(2)}) copy-start(s32[64,14]{1,0:T(8,128)S(1)} %copy.80) | copy-start | bytes 10756
  26.8 201.7 %copy-start.30 = (s32[64,14]{1,0:T(8,128)}, s32[64,14]{1,0:T(8,128)S(1)}, u32[]{:S(2)}) copy-start(s32[64,14]{1,0:T(8,128)S(1)} %copy.73) | copy-start | bytes 10756
  327.4 17.5 %copy-start.39 = (s32[64,14]{1,0:T(8,128)S(1)}, s32[64,14]{1,0:T(8,128)}, u32[]{:S(2)}) copy-start(s32[64,14]{1,0:T(8,128)} %copy-done.38) | copy-start | bytes 10756
  363.9 17.9 %copy-start.37 = (s32[64,14]{1,0:T(8,128)S(1)}, s32[64,14]{1,0:T(8,128)}, u32[]{:S(2)}) copy-start(s32[64,14]{1,0:T(8,128)} %copy-done.36) | copy-start | bytes 10756
  400.7 17.5 %copy-start.35 = (s32[64,14]{1,0:T(8,128)S(1)}, s32[64,14]{1,0:T(8,128)}, u32[]{:S(2)}) copy-start(s32[64,14]{1,0:T(8,128)} %copy-done.34) | copy-start | bytes 10756
  437.1 17.5 %copy-start.33 = (s32[64,14]{1,0:T(8,128)S(1)}, s32[64,14]{1,0:T(8,128)}, u32[]{:S(2)}) copy-start(s32[64,14]{1,0:T(8,128)} %copy-done.32) | copy-start | bytes 10756
  473.5 17.6 %copy-start.31 = (s32[64,14]{1,0:T(8,128)S(1)}, s32[64,14]{1,0:T(8,128)}, u32[]{:S(2)}) copy-start(s32[64,14]{1,0:T(8,128)} %copy-done.30) | copy-start | bytes 10756
  510.0 17.7 %copy-start.15 = (f32[64,14,32]{2,1,0:T(8,128)S(1)}, f32[64,14,32]{2,1,0:T(8,128)}, u32[]{:S(2)}) copy-start(f32[64,14,32]{2,1,0:T(8,128)} %get-tuple-element.54) | copy-start | bytes 344068
  510.0 17.7 %copy-start.51 = (f32[128]{0:T(128)S(1)}, f32[128]{0:T(128)}, u32[]{:S(2)}) copy-start(f32[128]{0:T(128)} %get-tuple-element.33) | copy-start | bytes 1540
  510.0 17.7 %copy-start.52 = (f32[128]{0:T(128)S(1)}, f32[128]{0:T(128)}, u32[]{:S(2)}) copy-start(f32[128]{0:T(128)} %get-tuple-element.34) | copy-start | bytes 1540
  510.0 17.7 %copy-start.53 = (f32[128]{0:T(128)S(1)}, f32[128]{0:T(128)}, u32[]{:S(2)}) copy-start(f32[128]{0:T(128)} %get-tuple-element.35) | copy-start | bytes 1540
  510.0 38.4 %slice-start = ((s8[14680064]{0:T(1024)(128)(4,1)}), s8[2097152]{0:T(1024)(128)(4,1)S(1)}, s32[]{:S(2)}) async-start(s8[14680064]{0:T(1024)(128)(4,1)} %bitcast.228), calls=%async_computation.2 | async-start | bytes 4194304
  527.7 20.8 %slice-start.1 = ((s8[14680064]{0:T(1024)(128)(4,1)}), s8[4194304]{0:T(1024)(128)(4,1)S(1)}, s32[]{:S(2)}) async-start(s8[14680064]{0:T(1024)(128)(4,1)} %bitcast.228), calls=%async_computation.3 | async-start | bytes 8388608
  527.7 20.8 %slice-start.2 = ((s8[14680064]{0:T(1024)(128)(4,1)}), s8[4194304]{0:T(1024)(128)(4,1)S(1)}, s32[]{:S(2)}) async-start(s8[14680064]{0:T(1024)(128)(4,1)} %bitcast.228), calls=%async_computation.4 | async-start | bytes 8388608
  527.7 20.8 %slice-start.3 = ((s8[14680064]{0:T(1024)(128)(4,1)}), s8[4194304]{0:T(1024)(128)(4,1)S(1)}, s32[]{:S(2)}) async-start(s8[14680064]{0:T(1024)(128)(4,1)} %bitcast.228), calls=%async_computation.5 | async-start | bytes 8388608
  527.7 20.8 %copy-start.17 = (f32[64,14,32]{2,1,0:T(8,128)S(1)}, f32[64,14,32]{2,1,0:T(8,128)}, u32[]{:S(2)}) copy-start(f32[64,14,32]{2,1,0:T(8,128)} %get-tuple-element.52) | copy-start | bytes 344068
  527.7 37.4 %slice-start.4 = ((s8[14680064]{0:T(1024)(128)(4,1)}), s8[4194304]{0:T(1024)(128)(4,1)S(1)}, s32[]{:S(2)}) async-start(s8[14680064]{0:T(1024)(128)(4,1)} %bitcast.241), calls=%async_computation.6 | async-start | bytes 8388608
  527.8 37.4 %slice-start.5 = ((s8[14680064]{0:T(1024)(128)(4,1)}), s8[4194304]{0:T(1024)(128)(4,1)S(1)}, s32[]{:S(2)}) async-start(s8[14680064]{0:T(1024)(128)(4,1)} %bitcast.241), calls=%async_computation.7 | async-start | bytes 8388608
  548.5 16.7 %slice-start.6 = ((s8[14680064]{0:T(1024)(128)(4,1)}), s8[4194304]{0:T(1024)(128)(4,1)S(1)}, s32[]{:S(2)}) async-start(s8[14680064]{0:T(1024)(128)(4,1)} %bitcast.241), calls=%async_computation.8 | async-start | bytes 8388608
  548.5 16.7 %slice-start.7 = ((s8[14680064]{0:T(1024)(128)(4,1)}), s8[2097152]{0:T(1024)(128)(4,1)S(1)}, s32[]{:S(2)}) async-start(s8[14680064]{0:T(1024)(128)(4,1)} %bitcast.241), calls=%async_computation.9 | async-start | bytes 4194304
  548.5 16.7 %copy-start.19 = (f32[64,14,32]{2,1,0:T(8,128)S(1)}, f32[64,14,32]{2,1,0:T(8,128)}, u32[]{:S(2)}) copy-start(f32[64,14,32]{2,1,0:T(8,128)} %get-tuple-element.50) | copy-start | bytes 344068
  565.2 10.9 %copy-start.21 = (f32[64,14,32]{2,1,0:T(8,128)S(1)}, f32[64,14,32]{2,1,0:T(8,128)}, u32[]{:S(2)}) copy-start(f32[64,14,32]{2,1,0:T(8,128)} %get-tuple-element.48) | copy-start | bytes 344068
  576.1 17.9 %copy-start.3 = (f32[64,14,32,128]{3,2,1,0:T(8,128)S(1)}, f32[64,14,32,128]{3,2,1,0:T(8,128)}, u32[]{:S(2)}) copy-start(f32[64,14,32,128]{3,2,1,0:T(8,128)} %reshape.362) | copy-start | bytes 44040196
  576.1 17.9 %copy-start.23 = (f32[64,14,32]{2,1,0:T(8,128)S(1)}, f32[64,14,32]{2,1,0:T(8,128)}, u32[]{:S(2)}) copy-start(f32[64,14,32]{2,1,0:T(8,128)} %get-tuple-element.46) | copy-start | bytes 344068
  594.0 10.9 %copy-start.25 = (f32[64,14,32]{2,1,0:T(8,128)S(1)}, f32[64,14,32]{2,1,0:T(8,128)}, u32[]{:S(2)}) copy-start(f32[64,14,32]{2,1,0:T(8,128)} %get-tuple-element.44) | copy-start | bytes 344068
  604.8 17.9 %copy-start.4 = (f32[64,14,32,128]{3,2,1,0:T(8,128)S(1)}, f32[64,14,32,128]{3,2,1,0:T(8,128)}, u32[]{:S(2)}) copy-start(f32[64,14,32,128]{3,2,1,0:T(8,128)} %reshape.360) | copy-start | bytes 44040196
  604.8 17.9 %copy-start.27 = (f32[64,14,32]{2,1,0:T(8,128)S(1)}, f32[64,14,32]{2,1,0:T(8,128)}, u32[]{:S(2)}) copy-start(f32[64,14,32]{2,1,0:T(8,128)} %get-tuple-element.42) | copy-start | bytes 344068
  622.7 10.9 %copy-start.29 = (f32[64,14,32]{2,1,0:T(8,128)S(1)}, f32[64,14,32]{2,1,0:T(8,128)}, u32[]{:S(2)}) copy-start(f32[64,14,32]{2,1,0:T(8,128)} %get-tuple-element.40) | copy-start | bytes 344068
  693.4 54.8 %all-to-all-start = ((bf16[2,64,224,128]{3,2,1,0:T(8,128)(2,1)}), bf16[2,64,224,128]{3,2,1,0:T(8,128)(2,1)}, u32[]{:S(2)}, u32[]{:S(2)}) async-start(bf16[2,64,224,128]{3,2,1,0:T(8,128)(2,1)} %pad_maximum_fusion.1), calls=%async_computation | async-start | bytes 14680064 | tf_op jit(solution)/shard_map/all_to_all | solution.py:145
  862.5 14.4 %copy-start.50 = (f32[2,128]{1,0:T(2,128)S(1)}, f32[2,128]{1,0:T(2,128)}, u32[]{:S(2)}) copy-start(f32[2,128]{1,0:T(2,128)} %param.21) | copy-start | bytes 3076
  862.5 14.5 %copy-start.48 = (bf16[256,128]{1,0:T(8,128)(2,1)S(1)}, bf16[256,128]{1,0:T(8,128)(2,1)}, u32[]{:S(2)}) copy-start(bf16[256,128]{1,0:T(8,128)(2,1)} %param.19) | copy-start | bytes 196612
  870.3 55.6 %all-to-all-start.1 = ((bf16[128,224,128]{2,1,0:T(8,128)(2,1)}), bf16[128,224,128]{2,1,0:T(8,128)(2,1)}, u32[]{:S(2)}, u32[]{:S(2)}) async-start(bf16[128,224,128]{2,1,0:T(8,128)(2,1)} %bitcast.240), calls=%async_computation.1 | async-start | bytes 14680064 | tf_op jit(solution)/shard_map/all_to_all | solution.py:149
  877.0 12.9 %copy-start.28 = (f32[64,14,32]{2,1,0:T(8,128)S(1)}, f32[64,14,32]{2,1,0:T(8,128)}, u32[]{:S(2)}) copy-start(f32[64,14,32]{2,1,0:T(8,128)} %get-tuple-element.42) | copy-start | bytes 344068
  877.0 12.9 %copy-start.44 = (f32[64,14,32]{2,1,0:T(8,128)S(1)}, f32[64,14,32]{2,1,0:T(8,128)}, u32[]{:S(2)}) copy-start(f32[64,14,32]{2,1,0:T(8,128)} %get-tuple-element.6) | copy-start | bytes 344068
  877.0 12.9 %copy-start.45 = (f32[64,14,32]{2,1,0:T(8,128)S(1)}, f32[64,14,32]{2,1,0:T(8,128)}, u32[]{:S(2)}) copy-start(f32[64,14,32]{2,1,0:T(8,128)} %get-tuple-element.7) | copy-start | bytes 344068
  877.0 14.1 %copy-start.24 = (f32[64,14,32]{2,1,0:T(8,128)S(1)}, f32[64,14,32]{2,1,0:T(8,128)}, u32[]{:S(2)}) copy-start(f32[64,14,32]{2,1,0:T(8,128)} %get-tuple-element.46) | copy-start | bytes 344068
  877.0 14.1 %copy-start.26 = (f32[64,14,32]{2,1,0:T(8,128)S(1)}, f32[64,14,32]{2,1,0:T(8,128)}, u32[]{:S(2)}) copy-start(f32[64,14,32]{2,1,0:T(8,128)} %get-tuple-element.44) | copy-start | bytes 344068
  877.0 14.1 %copy-start.42 = (f32[64,14,32]{2,1,0:T(8,128)S(1)}, f32[64,14,32]{2,1,0:T(8,128)}, u32[]{:S(2)}) copy-start(f32[64,14,32]{2,1,0:T(8,128)} %get-tuple-element.8) | copy-start | bytes 344068
  877.0 14.1 %copy-start.43 = (f32[64,14,32]{2,1,0:T(8,128)S(1)}, f32[64,14,32]{2,1,0:T(8,128)}, u32[]{:S(2)}) copy-start(f32[64,14,32]{2,1,0:T(8,128)} %get-tuple-element.9) | copy-start | bytes 344068
  877.0 15.5 %copy-start.20 = (f32[64,14,32]{2,1,0:T(8,128)S(1)}, f32[64,14,32]{2,1,0:T(8,128)}, u32[]{:S(2)}) copy-start(f32[64,14,32]{2,1,0:T(8,128)} %get-tuple-element.50) | copy-start | bytes 344068
  877.1 15.5 %copy-start.22 = (f32[64,14,32]{2,1,0:T(8,128)S(1)}, f32[64,14,32]{2,1,0:T(8,128)}, u32[]{:S(2)}) copy-start(f32[64,14,32]{2,1,0:T(8,128)} %get-tuple-element.48) | copy-start | bytes 344068
  877.1 15.5 %copy-start.40 = (f32[64,14,32]{2,1,0:T(8,128)S(1)}, f32[64,14,32]{2,1,0:T(8,128)}, u32[]{:S(2)}) copy-start(f32[64,14,32]{2,1,0:T(8,128)} %get-tuple-element.10) | copy-start | bytes 344068
  877.1 15.5 %copy-start.41 = (f32[64,14,32]{2,1,0:T(8,128)S(1)}, f32[64,14,32]{2,1,0:T(8,128)}, u32[]{:S(2)}) copy-start(f32[64,14,32]{2,1,0:T(8,128)} %get-tuple-element.11) | copy-start | bytes 344068
  877.1 16.8 %copy-start.16 = (f32[64,14,32]{2,1,0:T(8,128)S(1)}, f32[64,14,32]{2,1,0:T(8,128)}, u32[]{:S(2)}) copy-start(f32[64,14,32]{2,1,0:T(8,128)} %get-tuple-element.54) | copy-start | bytes 344068
  877.1 16.8 %copy-start.18 = (f32[64,14,32]{2,1,0:T(8,128)S(1)}, f32[64,14,32]{2,1,0:T(8,128)}, u32[]{:S(2)}) copy-start(f32[64,14,32]{2,1,0:T(8,128)} %get-tuple-element.52) | copy-start | bytes 344068
  877.1 18.2 %copy-start.7 = (f32[64,3,14,32]{3,2,1,0:T(8,128)S(1)}, f32[64,3,14,32]{3,2,1,0:T(8,128)}, u32[]{:S(2)}) copy-start(f32[64,3,14,32]{3,2,1,0:T(8,128)} %get-tuple-element.55) | copy-start | bytes 1032196
  877.1 18.2 %copy-start.8 = (f32[64,3,14,32]{3,2,1,0:T(8,128)S(1)}, f32[64,3,14,32]{3,2,1,0:T(8,128)}, u32[]{:S(2)}) copy-start(f32[64,3,14,32]{3,2,1,0:T(8,128)} %get-tuple-element.53) | copy-start | bytes 1032196
  877.1 18.1 %copy-start.9 = (f32[64,3,14,32]{3,2,1,0:T(8,128)S(1)}, f32[64,3,14,32]{3,2,1,0:T(8,128)}, u32[]{:S(2)}) copy-start(f32[64,3,14,32]{3,2,1,0:T(8,128)} %get-tuple-element.51) | copy-start | bytes 1032196
  877.1 18.1 %copy-start.10 = (f32[64,3,14,32]{3,2,1,0:T(8,128)S(1)}, f32[64,3,14,32]{3,2,1,0:T(8,128)}, u32[]{:S(2)}) copy-start(f32[64,3,14,32]{3,2,1,0:T(8,128)} %get-tuple-element.49) | copy-start | bytes 1032196
  877.1 18.1 %copy-start.11 = (f32[64,3,14,32]{3,2,1,0:T(8,128)S(1)}, f32[64,3,14,32]{3,2,1,0:T(8,128)}, u32[]{:S(2)}) copy-start(f32[64,3,14,32]{3,2,1,0:T(8,128)} %get-tuple-element.47) | copy-start | bytes 1032196
  877.2 18.1 %copy-start.12 = (f32[64,3,14,32]{3,2,1,0:T(8,128)S(1)}, f32[64,3,14,32]{3,2,1,0:T(8,128)}, u32[]{:S(2)}) copy-start(f32[64,3,14,32]{3,2,1,0:T(8,128)} %get-tuple-element.45) | copy-start | bytes 1032196
  877.2 18.1 %copy-start.13 = (f32[64,3,14,32]{3,2,1,0:T(8,128)S(1)}, f32[64,3,14,32]{3,2,1,0:T(8,128)}, u32[]{:S(2)}) copy-start(f32[64,3,14,32]{3,2,1,0:T(8,128)} %get-tuple-element.43) | copy-start | bytes 1032196
  877.2 18.1 %copy-start.14 = (f32[64,3,14,32]{3,2,1,0:T(8,128)S(1)}, f32[64,3,14,32]{3,2,1,0:T(8,128)}, u32[]{:S(2)}) copy-start(f32[64,3,14,32]{3,2,1,0:T(8,128)} %get-tuple-element.41) | copy-start | bytes 1032196
  895.3 37.7 %copy-start.54 = (bf16[128,128]{1,0:T(8,128)(2,1)S(1)}, bf16[128,128]{1,0:T(8,128)(2,1)}, u32[]{:S(2)}) copy-start(bf16[128,128]{1,0:T(8,128)(2,1)} %param.20) | copy-start | bytes 98308
  (6 other events, 49.7 us)
